TPU v7x, 256 devices: a whole 4x4x8 slice. The times are simulated.
256 devices in a mesh: member: 128 (over y, z, x), pair: 2 (over core).
Axes of the slice: x: 4, y: 4, z: 8, core: 2. Of those that a mesh axis runs over, the one named last changes fastest.
Arguments:
- samples: bfloat16 [512, 512], replicated, may hold values from -6 to 6
- w_first: bfloat16 [128, 512, 2048], P('member', None, 'pair'), may hold values from -6 to 6
- b_first: bfloat16 [128, 2048], P('member', 'pair'), may hold values from -6 to 6
- w_second: bfloat16 [128, 2048, 2048], P('member', None, 'pair'), may hold values from -6 to 6
- b_second: bfloat16 [128, 2048], P('member', 'pair'), may hold values from -6 to 6
- w_third: bfloat16 [128, 2048, 64], P('member', 'pair'), may hold values from -6 to 6
- observed: float32 [512, 64], replicated, may hold values from -24 to 24
- perturb: float32 [128, 512, 64], P('member'), may hold values from -6 to 6
- variance: float32 [512, 64], replicated, may hold values from 32 to 1024
Outputs:
- new_first: bfloat16 [128, 512, 2048], P('member', None, 'pair')
- new_bfirst: bfloat16 [128, 2048], P('member', 'pair')
- new_second: bfloat16 [128, 2048, 2048], P('member', None, 'pair')
- new_bsecond: bfloat16 [128, 2048], P('member', 'pair')
- new_third: bfloat16 [128, 2048, 64], P('member', 'pair')
All inputs are finite; a program needn't handle non-finite values.
Results may differ from a plain program's by a relative error of at most 0.019.
Values may be sent and summed in bfloat16 or wider, within the bound.
A program may use at most 128 MiB of HBM per device.

v0:
```python
import jax
import jax.numpy as jnp
from jax import lax
from jax.sharding import PartitionSpec as P


def solve_gain(amat, bmat):
    count = amat.shape[0]
    system = amat + count * jnp.eye(count, dtype=jnp.float32)
    factor = jnp.linalg.cholesky(system)
    middle = lax.linalg.triangular_solve(
        factor, bmat, left_side=True, lower=True, transpose_a=False
    )
    return lax.linalg.triangular_solve(factor, middle, left_side=True, lower=True, transpose_a=True)


def moments(allpred, allres, var_cols):
    devpred = allpred - jnp.mean(allpred, axis=0, keepdims=True)
    scaled = devpred / var_cols
    amat = jnp.dot(scaled, devpred.T, precision=lax.Precision.HIGHEST)
    bmat = jnp.dot(scaled, allres.T, precision=lax.Precision.HIGHEST)
    return (amat, bmat)


def to_slabs(shards):
    flats = [piece.reshape(1, -1) for piece in shards]
    return (
        lax.all_to_all(flats[0], "member", split_axis=1, concat_axis=0, tiled=True),
        lax.all_to_all(flats[1], "member", split_axis=1, concat_axis=0, tiled=True),
        lax.all_to_all(flats[2], "member", split_axis=1, concat_axis=0, tiled=True),
        lax.all_to_all(flats[3], "member", split_axis=1, concat_axis=0, tiled=True),
        lax.all_to_all(flats[4], "member", split_axis=1, concat_axis=0, tiled=True),
    )


def mix_slab(slab, gain_tr):
    full = slab.astype(jnp.float32)
    center = (full - jnp.mean(full, axis=0, keepdims=True)).astype(jnp.bfloat16)
    return jnp.dot(gain_tr, center, preferred_element_type=jnp.float32).astype(jnp.bfloat16)


def body(samples, w_first, b_first, w_second, b_second, w_third, observed, perturb, variance):
    shards = (w_first, b_first, w_second, b_second, w_third)
    in_scale = samples.shape[1] ** (-0.5)
    hid_scale = w_second.shape[1] ** (-0.5)
    first = jax.nn.gelu(
        jnp.dot(samples, w_first[0], preferred_element_type=jnp.float32) * in_scale
        + b_first[0].astype(jnp.float32),
        approximate=True,
    ).astype(jnp.bfloat16)
    second_w = w_second[0]
    summed = jnp.dot(
        lax.all_gather(first, "pair", axis=1, tiled=True),
        second_w,
        preferred_element_type=jnp.float32,
    )
    second = jax.nn.gelu(
        summed * hid_scale + b_second[0].astype(jnp.float32), approximate=True
    ).astype(jnp.bfloat16)
    partial_out = jnp.dot(second, w_third[0], preferred_element_type=jnp.float32) * hid_scale
    pred = lax.psum(partial_out, "pair")
    resid = observed + jnp.sqrt(variance) * perturb[0] - pred
    half = pred.shape[0] // 2
    row_start = lax.axis_index("pair") * half
    pred_half = lax.dynamic_slice_in_dim(pred, row_start, half, 0).reshape(1, -1)
    res_half = lax.dynamic_slice_in_dim(resid, row_start, half, 0).reshape(1, -1)
    var_half = lax.dynamic_slice_in_dim(variance, row_start, half, 0).reshape(1, -1)
    allpred, allres = (
        lax.all_gather(pred_half, "member", axis=0, tiled=True),
        lax.all_gather(res_half, "member", axis=0, tiled=True),
    )
    amat, bmat = moments(allpred, allres, var_half)
    amat, bmat = lax.psum((amat, bmat), "pair")
    gain = solve_gain(amat, bmat)
    gain_tr = gain.astype(jnp.bfloat16).T
    slabs = to_slabs(shards)
    mixed = [mix_slab(slab, gain_tr) for slab in slabs]
    returned = (
        lax.all_to_all(mixed[0], "member", split_axis=0, concat_axis=1, tiled=True),
        lax.all_to_all(mixed[1], "member", split_axis=0, concat_axis=1, tiled=True),
        lax.all_to_all(mixed[2], "member", split_axis=0, concat_axis=1, tiled=True),
        lax.all_to_all(mixed[3], "member", split_axis=0, concat_axis=1, tiled=True),
        lax.all_to_all(mixed[4], "member", split_axis=0, concat_axis=1, tiled=True),
    )
    return tuple((back.reshape(orig.shape) for back, orig in zip(returned, shards)))


def solution(mesh):
    in_specs = (
        P(),
        P("member", None, "pair"),
        P("member", "pair"),
        P("member", None, "pair"),
        P("member", "pair"),
        P("member", "pair", None),
        P(),
        P("member", None, None),
        P(),
    )
    out_specs = (
        P("member", None, "pair"),
        P("member", "pair"),
        P("member", None, "pair"),
        P("member", "pair"),
        P("member", "pair", None),
    )
    return jax.shard_map(body, mesh=mesh, in_specs=in_specs, out_specs=out_specs, check_vma=False)
```

profile of v0, /device:TPU:30, one launch (start us, length us, event | category | flops | bytes accessed | tf_op | source)
XLA Modules:
  0.0 749.6 jit_solution(3870026688154585423)
XLA Ops:
  11.8 18.6 %all-gather.6.cloned.1.call-done = bf16[512,2048]{1,0:T(8,128)(2,1)} async-done(((bf16[512,1024]{1,0:T(8,128)(2,1)}), bf16[512,2048]{1,0:T(8,128)(2,1)}) %all-gather.6.cloned.1.call-update) | async-done | bytes 2097168 | tf_op jit(solution)/shard_map/all_gather | solution.py:53
  37.0 30.1 %all-reduce.4.cloned.1.call-done = f32[512,64]{0,1:T(8,128)} async-done(((f32[512,64]{0,1:T(8,128)}), f32[512,64]{0,1:T(8,128)}) %all-reduce.4.cloned.1.call-update) | async-done | bytes 131088 | tf_op jit(solution)/shard_map/psum | solution.py:61
  70.6 14.2 %all-to-all-start.2 = ((bf16[1,128,8]{2,0,1:T(2,128)(2,1)}), bf16[1,128,8]{2,0,1:T(2,128)(2,1)S(1)}, u32[]{:S(2)}, u32[]{:S(2)}) async-start(bf16[1,128,8]{2,0,1:T(2,128)(2,1)} %all_to_all.127), calls=%async_computation.2 | async-start | bytes 131072 | tf_op jit(solution)/shard_map/all_to_all | solution.py:29
  110.7 19.7 %all-to-all-start.8 = ((bf16[128,2,256]{2,1,0:T(2,128)(2,1)}), bf16[128,2,256]{2,1,0:T(2,128)(2,1)S(1)}, u32[]{:S(2)}, u32[]{:S(2)}) async-start(bf16[128,2,256]{2,1,0:T(2,128)(2,1)} %reshape.164), calls=%async_computation.8 | async-start | bytes 262144 | tf_op jit(solution)/shard_map/all_to_all | solution.py:32
  145.3 13.8 %all-to-all-start = ((bf16[128,2,2048]{2,1,0:T(2,128)(2,1)}), bf16[128,2,2048]{2,1,0:T(2,128)(2,1)S(1)}, u32[]{:S(2)}, u32[]{:S(2)}) async-start(bf16[128,2,2048]{2,1,0:T(2,128)(2,1)} %reshape.156), calls=%async_computation | async-start | bytes 2097152 | tf_op jit(solution)/shard_map/all_to_all | solution.py:28
  159.1 19.6 %all_to_all.128 = bf16[1,128,16384]{2,0,1:T(2,128)(2,1)} reshape(bf16[1,2048,1024]{2,1,0:T(8,128)(2,1)} %param.12) | data formatting | bytes 8388608 | tf_op jit(solution)/shard_map/all_to_all | solution.py:30
  178.7 26.8 %reduce.23 = bf16[128,16384]{1,0:T(8,128)(2,1)} reduce(bf16[128,1,16384]{2,1,0:T(2,128)(2,1)} %bitcast.88, bf16[]{:T(256)} %broadcast.159), dimensions={1}, to_apply=%bitcast.69.reduce_sub_computation | reduce | bytes 8388610
  214.2 14.2 %all-to-all-start.4 = ((bf16[128,2,8192]{2,1,0:T(2,128)(2,1)}), bf16[128,2,8192]{2,1,0:T(2,128)(2,1)}, u32[]{:S(2)}, u32[]{:S(2)}) async-start(bf16[128,2,8192]{2,1,0:T(2,128)(2,1)} %reshape.160), calls=%async_computation.4 | async-start | bytes 8388608 | tf_op jit(solution)/shard_map/all_to_all | solution.py:30
  247.0 107.1 %all-gather.10.cloned.1.call-done = f32[128,1,16384]{2,1,0:T(1,128)} async-done(((f32[1,1,16384]{2,1,0:T(1,128)}), f32[128,1,16384]{2,1,0:T(1,128)}) %all-gather.10.cloned.1.call-update) | async-done | bytes 8388624 | tf_op jit(solution)/shard_map/all_gather | solution.py:70
  354.1 21.6 %fusion.2 = f32[128,128]{1,0:T(8,128)} fusion(f32[128,1,16384]{2,1,0:T(1,128)} %all-gather.10.cloned.1.call-done, f32[128,1,16384]{2,1,0:T(1,128)} %all-gather.8.cloned.1.call-done, f32[16384]{0:T(1024)S(1)} %div.43, f32[16384]{0:T(1024)S(1)} %broadcast_multiply_fusion.1), kind=kOutput, calls=%fused_computation.4 | convolution fusion | flops 3225419776 | bytes 16973824 | tf_op jit(solution)/shard_map/dot_general | solution.py:21
  375.8 21.6 %fusion.6 = f32[128,128]{1,0:T(8,128)} fusion(f32[128,1,16384]{2,1,0:T(1,128)} %all-gather.8.cloned.1.call-done, f32[16384]{0:T(1024)S(1)} %div.43, f32[16384]{0:T(1024)S(1)} %broadcast_multiply_fusion.1), kind=kOutput, calls=%fused_computation.9 | convolution fusion | flops 3227516928 | bytes 8585216 | tf_op jit(solution)/shard_map/dot_general | solution.py:20
  399.8 25.1 %all-reduce.6.cloned.1.call-done = (f32[128,128]{1,0:T(8,128)}, f32[128,128]{1,0:T(8,128)}) async-done(((f32[128,128]{1,0:T(8,128)}, f32[128,128]{1,0:T(8,128)}), (f32[128,128]{1,0:T(8,128)}, f32[128,128]{1,0:T(8,128)})) %all-reduce.6.cloned.1.call-update) | async-done | bytes 131088 | tf_op jit(solution)/shard_map/psum | solution.py:73
  426.7 11.7 %cholesky.16 = f32[128,128]{1,0:T(8,128)S(1)} custom-call(f32[128,128]{1,0:T(8,128)S(1)} %fusion.63), custom_call_target="Cholesky" | custom-call | tf_op jit(solution)/shard_map/jit(cholesky)/cholesky | solution.py:10
  439.7 9.8 %custom-call.8 = f32[1,128,128]{1,2,0:T(8,128)S(1)} custom-call(f32[1,128,128]{2,1,0:T(8,128)S(1)} %fusion.58), custom_call_target="InvertDiagBlocksLowerTriangular" | custom-call | tf_op jit(solution)/shard_map/triangular_solve | solution.py:14
  451.8 14.2 %all-to-all-start.3 = ((bf16[128,1,8]{2,1,0:T(2,128)(2,1)}), bf16[128,1,8]{2,1,0:T(2,128)(2,1)S(1)}, u32[]{:S(2)}, u32[]{:S(2)}) async-start(bf16[128,1,8]{2,1,0:T(2,128)(2,1)} %copy.45), calls=%async_computation.3 | async-start | bytes 131072 | tf_op jit(solution)/shard_map/all_to_all | solution.py:80
  474.2 9.9 %all-to-all-start.7 = ((bf16[128,1,8]{2,1,0:T(2,128)(2,1)}), bf16[128,1,8]{2,1,0:T(2,128)(2,1)S(1)}, u32[]{:S(2)}, u32[]{:S(2)}) async-start(bf16[128,1,8]{2,1,0:T(2,128)(2,1)} %copy.49), calls=%async_computation.7 | async-start | bytes 131072 | tf_op jit(solution)/shard_map/all_to_all | solution.py:82
  492.2 9.7 %all-to-all-start.9 = ((bf16[128,2,256]{2,1,0:T(2,128)(2,1)}), bf16[128,2,256]{2,1,0:T(2,128)(2,1)S(1)}, u32[]{:S(2)}, u32[]{:S(2)}) async-start(bf16[128,2,256]{2,1,0:T(2,128)(2,1)} %reshape.166), calls=%async_computation.9 | async-start | bytes 262144 | tf_op jit(solution)/shard_map/all_to_all | solution.py:83
  501.9 19.9 %reshape.161 = bf16[128,1,16384]{2,1,0:T(2,128)(2,1)} reshape(bf16[128,2,8192]{2,1,0:T(2,128)(2,1)} %all-to-all-done.4) | data formatting | bytes 8388608
  528.5 14.3 %all-to-all-start.1 = ((bf16[128,2,2048]{2,1,0:T(2,128)(2,1)}), bf16[128,2,2048]{2,1,0:T(2,128)(2,1)S(1)}, u32[]{:S(2)}, u32[]{:S(2)}) async-start(bf16[128,2,2048]{2,1,0:T(2,128)(2,1)} %reshape.158), calls=%async_computation.1 | async-start | bytes 2097152 | tf_op jit(solution)/shard_map/all_to_all | solution.py:79
  542.8 10.0 %bitcast_convert_fusion = f32[1,128,16384]{2,0,1:T(1,128)S(1)} fusion(bf16[128,1,16384]{2,1,0:T(2,128)(2,1)} %reshape.161), kind=kLoop, calls=%fused_computation.100 | loop fusion | flops 2097152 | bytes 12582912 | tf_op jit(solution)/shard_map/convert_element_type | solution.py:37
  584.8 14.6 %all-to-all-start.5 = ((bf16[128,2,8192]{2,1,0:T(2,128)(2,1)}), bf16[128,2,8192]{2,1,0:T(2,128)(2,1)}, u32[]{:S(2)}, u32[]{:S(2)}) async-start(bf16[128,2,8192]{2,1,0:T(2,128)(2,1)} %reshape.162), calls=%async_computation.5 | async-start | bytes 8388608 | tf_op jit(solution)/shard_map/all_to_all | solution.py:81
  619.4 70.3 %all-to-all-done.5 = bf16[128,2,8192]{2,1,0:T(2,128)(2,1)} async-done(((bf16[128,2,8192]{2,1,0:T(2,128)(2,1)}), bf16[128,2,8192]{2,1,0:T(2,128)(2,1)}, u32[]{:S(2)}, u32[]{:S(2)}) %all-to-all-start.5) | async-done | bytes 4194336 | tf_op jit(solution)/shard_map/all_to_all | solution.py:81
  689.7 19.8 %reshape.163 = bf16[128,1,16384]{2,1,0:T(2,128)(2,1)} reshape(bf16[128,2,8192]{2,1,0:T(2,128)(2,1)} %all-to-all-done.5) | data formatting | bytes 8388608
  709.4 26.1 %reduce.15 = bf16[128,16384]{1,0:T(8,128)(2,1)} reduce(bf16[128,1,16384]{2,1,0:T(2,128)(2,1)} %reshape.163, bf16[]{:T(256)} %constant.88), dimensions={1}, to_apply=%all_to_all.116.reduce_sub_computation | reduce | bytes 8388610 | tf_op jit(solution)/shard_map/all_to_all | solution.py:81
  (111 shorter events, 172.5 us)
Async XLA Ops:
  7.2 1.1 copy-start
  7.2 23.3 %all-gather.6.cloned.1.call-start = ((), (), s32[]{:S(2)}) async-start(), calls=%async_computation.10 | async-start | bytes 3145728 | tf_op jit(solution)/shard_map/all_gather | solution.py:53
  8.3 22.2 %copy-start.5 = (bf16[1,1024,64]{1,2,0:T(8,128)(2,1)S(1)}, bf16[1,1024,64]{1,2,0:T(8,128)(2,1)}, u32[]{:S(2)}) copy-start(bf16[1,1024,64]{1,2,0:T(8,128)(2,1)} %param.14) | copy-start | bytes 393220
  11.8 55.4 %all-reduce.4.cloned.1.call-start = ((), (), s32[]{:S(2)}) async-start(), calls=%async_computation.11 | async-start | bytes 262144 | tf_op jit(solution)/shard_map/psum | solution.py:61
  30.5 36.7 %copy-start.6 = (f32[512,64]{0,1:T(8,128)S(1)}, f32[512,64]{0,1:T(8,128)}, u32[]{:S(2)}) copy-start(f32[512,64]{0,1:T(8,128)} %param.17) | copy-start | bytes 393220
  30.5 36.7 %copy-start.7 = (f32[1,512,64]{1,2,0:T(8,128)S(1)}, f32[1,512,64]{1,2,0:T(8,128)}, u32[]{:S(2)}) copy-start(f32[1,512,64]{1,2,0:T(8,128)} %param.16) | copy-start | bytes 393220
  30.5 36.7 %copy-start.8 = (f32[512,64]{0,1:T(8,128)S(1)}, f32[512,64]{0,1:T(8,128)}, u32[]{:S(2)}) copy-start(f32[512,64]{0,1:T(8,128)} %param.15) | copy-start | bytes 393220
  37.0 203.3 %all-gather.8.cloned.1.call-start = ((), (), s32[]{:S(2)}) async-start(), calls=%async_computation.12 | async-start | bytes 8454144 | tf_op jit(solution)/shard_map/all_gather | solution.py:69
  68.9 285.2 %all-gather.10.cloned.1.call-start = ((), (), s32[]{:S(2)}) async-start(), calls=%async_computation.13 | async-start | bytes 8454144 | tf_op jit(solution)/shard_map/all_gather | solution.py:70
  70.6 22.3 %all-to-all-start.2 = ((bf16[1,128,8]{2,0,1:T(2,128)(2,1)}), bf16[1,128,8]{2,0,1:T(2,128)(2,1)S(1)}, u32[]{:S(2)}, u32[]{:S(2)}) async-start(bf16[1,128,8]{2,0,1:T(2,128)(2,1)} %all_to_all.127), calls=%async_computation.2 | async-start | bytes 131072 | tf_op jit(solution)/shard_map/all_to_all | solution.py:29
  92.9 17.8 %all-to-all-start.6 = ((bf16[1,128,8]{2,0,1:T(2,128)(2,1)}), bf16[1,128,8]{2,0,1:T(2,128)(2,1)S(1)}, u32[]{:S(2)}, u32[]{:S(2)}) async-start(bf16[1,128,8]{2,0,1:T(2,128)(2,1)} %all_to_all.129), calls=%async_computation.6 | async-start | bytes 131072 | tf_op jit(solution)/shard_map/all_to_all | solution.py:31
  110.7 34.6 %all-to-all-start.8 = ((bf16[128,2,256]{2,1,0:T(2,128)(2,1)}), bf16[128,2,256]{2,1,0:T(2,128)(2,1)S(1)}, u32[]{:S(2)}, u32[]{:S(2)}) async-start(bf16[128,2,256]{2,1,0:T(2,128)(2,1)} %reshape.164), calls=%async_computation.8 | async-start | bytes 262144 | tf_op jit(solution)/shard_map/all_to_all | solution.py:32
  145.3 68.0 %all-to-all-start = ((bf16[128,2,2048]{2,1,0:T(2,128)(2,1)}), bf16[128,2,2048]{2,1,0:T(2,128)(2,1)S(1)}, u32[]{:S(2)}, u32[]{:S(2)}) async-start(bf16[128,2,2048]{2,1,0:T(2,128)(2,1)} %reshape.156), calls=%async_computation | async-start | bytes 2097152 | tf_op jit(solution)/shard_map/all_to_all | solution.py:28
  213.2 1.0 copy-start.4
  214.2 237.6 %all-to-all-start.4 = ((bf16[128,2,8192]{2,1,0:T(2,128)(2,1)}), bf16[128,2,8192]{2,1,0:T(2,128)(2,1)}, u32[]{:S(2)}, u32[]{:S(2)}) async-start(bf16[128,2,8192]{2,1,0:T(2,128)(2,1)} %reshape.160), calls=%async_computation.4 | async-start | bytes 8388608 | tf_op jit(solution)/shard_map/all_to_all | solution.py:30
  228.4 196.4 %all-reduce.6.cloned.1.call-start = ((), (), s32[]{:S(2)}) async-start(), calls=%async_computation.14 | async-start | bytes 262144 | tf_op jit(solution)/shard_map/psum | solution.py:73
  451.8 22.3 %all-to-all-start.3 = ((bf16[128,1,8]{2,1,0:T(2,128)(2,1)}), bf16[128,1,8]{2,1,0:T(2,128)(2,1)S(1)}, u32[]{:S(2)}, u32[]{:S(2)}) async-start(bf16[128,1,8]{2,1,0:T(2,128)(2,1)} %copy.45), calls=%async_computation.3 | async-start | bytes 131072 | tf_op jit(solution)/shard_map/all_to_all | solution.py:80
  474.2 18.0 %all-to-all-start.7 = ((bf16[128,1,8]{2,1,0:T(2,128)(2,1)}), bf16[128,1,8]{2,1,0:T(2,128)(2,1)S(1)}, u32[]{:S(2)}, u32[]{:S(2)}) async-start(bf16[128,1,8]{2,1,0:T(2,128)(2,1)} %copy.49), calls=%async_computation.7 | async-start | bytes 131072 | tf_op jit(solution)/shard_map/all_to_all | solution.py:82
  492.2 36.3 %all-to-all-start.9 = ((bf16[128,2,256]{2,1,0:T(2,128)(2,1)}), bf16[128,2,256]{2,1,0:T(2,128)(2,1)S(1)}, u32[]{:S(2)}, u32[]{:S(2)}) async-start(bf16[128,2,256]{2,1,0:T(2,128)(2,1)} %reshape.166), calls=%async_computation.9 | async-start | bytes 262144 | tf_op jit(solution)/shard_map/all_to_all | solution.py:83
  501.9 19.9 %copy-start.2 = (f32[1,128,4096]{2,0,1:T(1,128)S(1)}, f32[1,128,4096]{2,0,1:T(1,128)}, u32[]{:S(2)}) copy-start(f32[1,128,4096]{2,0,1:T(1,128)} %bitcast_convert_fusion.1) | copy-start | bytes 6291460
  528.5 55.3 %all-to-all-start.1 = ((bf16[128,2,2048]{2,1,0:T(2,128)(2,1)}), bf16[128,2,2048]{2,1,0:T(2,128)(2,1)S(1)}, u32[]{:S(2)}, u32[]{:S(2)}) async-start(bf16[128,2,2048]{2,1,0:T(2,128)(2,1)} %reshape.158), calls=%async_computation.1 | async-start | bytes 2097152 | tf_op jit(solution)/shard_map/all_to_all | solution.py:79
  583.8 1.0 copy-start.3
  584.8 104.9 %all-to-all-start.5 = ((bf16[128,2,8192]{2,1,0:T(2,128)(2,1)}), bf16[128,2,8192]{2,1,0:T(2,128)(2,1)}, u32[]{:S(2)}, u32[]{:S(2)}) async-start(bf16[128,2,8192]{2,1,0:T(2,128)(2,1)} %reshape.162), calls=%async_computation.5 | async-start | bytes 8388608 | tf_op jit(solution)/shard_map/all_to_all | solution.py:81
  709.4 33.4 %copy-start.1 = (bf16[512,512]{1,0:T(8,128)(2,1)S(1)}, bf16[512,512]{1,0:T(8,128)(2,1)}, u32[]{:S(2)}) copy-start(bf16[512,512]{1,0:T(8,128)(2,1)} %param.9) | copy-start | bytes 1572868
Sparse Core Ops, SparseCore 0:
  11.9 18.5 all-gather.5
  37.1 29.9 all-reduce.3
  70.8 139.4 all-gather.7
  213.7 140.3 all-gather.9
  397.5 27.2 all-reduce.5
where the time goes:
time: 764 us; the launch traced here: 750 us
  waiting for transfers between devices  277 us (36%)
  other arithmetic  140 us (18%)
  starting transfers between devices  135 us (18%)
  local copies, waits for them, and re-layouts  118 us (15%)
  matrix products  64.9 us (8%)
  between operations  14.3 us (2%)
    all_gather x1, waiting for transfers between devices, body(): lax.all_gather(res_half, 'member', axis=0, tiled=True)  107 us
    unnamed x35, local copies, waits for them, and re-layouts  79.3 us
    all_to_all x1, waiting for transfers between devices, body(): lax.all_to_all(mixed[2], 'member', split_axis=0, concat_axis=1, tiled=True)  70.3 us
    unnamed x4, other arithmetic  37 us
    all_to_all x2, other arithmetic, body(): lax.all_to_all(mixed[2], 'member', split_axis=0, concat_axis=1, tiled=True)  32.7 us
    psum x1, waiting for transfers between devices, body(): pred = lax.psum(partial_out, 'pair')  30.1 us
    psum x1, waiting for transfers between devices, body(): amat, bmat = lax.psum((amat, bmat), 'pair')  25.1 us
    dot_general x1, matrix products, moments(): bmat = jnp.dot(scaled, allres.T, precision=lax.Precision.HIGHEST)  21.6 us
  transfers between devices with their start and end apart: 15, of which 9 were waited for; matrix products, arithmetic and copies ran while one was open for 30% of the time, Pallas kernels for 0%

commit v1 on v0

--- a/solution.py
+++ b/solution.py
@@ -1,7 +1,304 @@
+import functools
+
 import jax
 import jax.numpy as jnp
 from jax import lax
+from jax.experimental import pallas as pl
+from jax.experimental.pallas import tpu as pltpu
 from jax.sharding import PartitionSpec as P
+
+MESH = pl.DeviceIdType.MESH
+ROWS = 16
+LANES = 128
+
+
+def holder(e):
+    y, x = e // 8, lax.rem(e // 2, 4)
+    return y * 32 + (lax.rem(x + y, 4) + 4 * lax.rem(e, 2)) * 4 + x
+
+
+def own_tile(me):
+    y, z, x = me // 32, lax.rem(me // 4, 8), lax.rem(me, 4)
+    return lax.rem(z, 4) == lax.rem(x + y, 4), y * 8 + x * 2 + z // 4
+
+
+BIAS_AT = 4
+
+
+def exchange_kernel(
+    members,
+    gain_tr,
+    w_first,
+    w_second,
+    w_third,
+    bias,
+    new_first,
+    new_second,
+    new_third,
+    new_bias,
+    slab,
+    mixed,
+    weights,
+    spread,
+    avg,
+    send_sem,
+    recv_sem,
+    send_extra,
+    recv_extra,
+    back_send,
+    back_extra,
+    back_recv,
+):
+    me, core = lax.axis_index("member"), lax.axis_index("pair")
+    y = pltpu.get_barrier_semaphore()
+    wide = w_second.shape[1]
+    narrow = w_first.shape[1] // 4
+    main = wide + narrow
+    holds, tile = own_tile(me)
+    mine = pl.ds(pl.multiple_of(me * ROWS, ROWS), ROWS)
+
+    def greet(i, _):
+        peer = lax.rem(me + i, members)
+        pl.semaphore_signal(y, inc=1, device_id=(peer, core), device_id_type=MESH)
+        return 0
+
+    lax.fori_loop(1, members, greet, 0)
+    pl.semaphore_wait(y, members - 1)
+
+    def rows_of(p):
+        return pl.ds(pl.multiple_of(p * ROWS, ROWS), ROWS)
+
+    def first_part(p):
+        return (
+            pl.ds(pl.multiple_of((p // 4) * ROWS, ROWS), ROWS),
+            pl.ds(pl.multiple_of(lax.rem(p, 4) * narrow, narrow), narrow),
+        )
+
+    def third_part(e):
+        return (
+            pl.ds(pl.multiple_of((e // 8) * ROWS, ROWS), ROWS),
+            pl.ds(pl.multiple_of(lax.rem(e, 8) * LANES, LANES), LANES),
+        )
+
+    def remote(src, dst, send, recv, peer):
+        return pltpu.make_async_remote_copy(
+            src_ref=src,
+            dst_ref=dst,
+            send_sem=send,
+            recv_sem=recv,
+            device_id=(peer, core),
+            device_id_type=MESH,
+        )
+
+    cols_second, cols_first, cols_extra = pl.ds(0, wide), pl.ds(wide, narrow), pl.ds(main, LANES)
+
+    def push(i, _):
+        p = lax.rem(me + i, members)
+        remote(w_second.at[rows_of(p), :], slab.at[mine, cols_second], send_sem, recv_sem, p).start()
+        remote(w_first.at[first_part(p)], slab.at[mine, cols_first], send_sem, recv_sem, p).start()
+        return 0
+
+    lax.fori_loop(1, members, push, 0)
+    pltpu.make_async_copy(w_second.at[mine, :], slab.at[mine, cols_second], recv_sem).start()
+    pltpu.make_async_copy(w_first.at[first_part(me)], slab.at[mine, cols_first], recv_sem).start()
+
+    def push_extra(e, _):
+        p = holder(e)
+        here = p == me
+
+        @pl.when(here)
+        def _():
+            pltpu.make_async_copy(
+                w_third.at[third_part(e)], slab.at[mine, cols_extra], recv_extra
+            ).start()
+
+        @pl.when(jnp.logical_not(here))
+        def _():
+            remote(
+                w_third.at[third_part(e)], slab.at[mine, cols_extra], send_extra, recv_extra, p
+            ).start()
+
+        return 0
+
+    lax.fori_loop(0, 32, push_extra, 0)
+
+    @pl.when(me == BIAS_AT)
+    def _():
+        pltpu.make_async_copy(bias, slab.at[mine, cols_extra], recv_extra).start()
+
+    @pl.when(me != BIAS_AT)
+    def _():
+        remote(bias, slab.at[mine, cols_extra], send_extra, recv_extra, BIAS_AT).start()
+
+    extra_here = jnp.logical_or(holds, me == BIAS_AT)
+
+    count = members * ROWS
+    at = lax.broadcasted_iota(jnp.int32, (members, count), 1) // ROWS
+    who = lax.broadcasted_iota(jnp.int32, (members, count), 0)
+    spread[...] = jnp.where(at == who, 1.0, 0.0).astype(jnp.bfloat16)
+
+    pltpu.make_async_copy(
+        slab.at[:, pl.ds(0, main)], slab.at[:, pl.ds(0, main)], recv_sem
+    ).wait()
+
+    @pl.when(extra_here)
+    def _():
+        pltpu.make_async_copy(slab.at[:, cols_extra], slab.at[:, cols_extra], recv_extra).wait()
+
+    group = weights.shape[0]
+    peers = group // ROWS
+
+    total = main + LANES
+    tr = lax.broadcasted_iota(jnp.int32, (ROWS, count), 1) % ROWS
+    tw = lax.broadcasted_iota(jnp.int32, (ROWS, count), 0)
+    same = jnp.where(tr == tw, 1.0, 0.0).astype(jnp.bfloat16)
+
+    @pl.loop(0, total // LANES)
+    def _(n):
+        c = pl.ds(pl.multiple_of(n * LANES, LANES), LANES)
+        avg[:, c] = jnp.dot(same, slab[:, c], preferred_element_type=jnp.float32) * (1.0 / members)
+
+    @pl.loop(0, members // peers)
+    def _(g):
+        jr = lax.broadcasted_iota(jnp.int32, (group, members), 0) // ROWS + g * peers
+        jj = lax.broadcasted_iota(jnp.int32, (group, members), 1)
+        pick = jnp.where(jr == jj, 1.0, 0.0).astype(jnp.bfloat16)
+        rep = jnp.dot(pick, gain_tr[...], preferred_element_type=jnp.float32)
+        weight_sum = jnp.sum(rep, axis=1, keepdims=True)
+        rep16 = rep.astype(jnp.bfloat16)
+
+        @pl.loop(0, count // 512)
+        def _(q):
+            c = pl.ds(pl.multiple_of(q * 512, 512), 512)
+            full = jnp.dot(rep16, spread[:, c], preferred_element_type=jnp.float32)
+            r0 = lax.broadcasted_iota(jnp.int32, (group, 512), 0) % ROWS
+            r1 = lax.broadcasted_iota(jnp.int32, (group, 512), 1) % ROWS
+            weights[:, c] = jnp.where(r0 == r1, full, 0.0).astype(jnp.bfloat16)
+
+        out_rows = pl.ds(pl.multiple_of(g * group, group), group)
+
+        def mix(c, width):
+            acc = jnp.dot(weights[...], slab[:, c], preferred_element_type=jnp.float32)
+            means = jnp.broadcast_to(avg[:, c][None], (peers, ROWS, width)).reshape(group, width)
+            mixed[out_rows, c] = (acc - weight_sum * means).astype(jnp.bfloat16)
+
+        @pl.loop(0, main // 256)
+        def _(n):
+            mix(pl.ds(pl.multiple_of(n * 256, 256), 256), 256)
+
+        @pl.when(extra_here)
+        def _():
+            mix(cols_extra, LANES)
+
+        def back(i, _):
+            j = g * peers + i
+            here = j == me
+
+            @pl.when(here)
+            def _():
+                pltpu.make_async_copy(
+                    mixed.at[mine, cols_second], new_second.at[mine, :], back_recv.at[0]
+                ).start()
+                pltpu.make_async_copy(
+                    mixed.at[mine, cols_first], new_first.at[first_part(me)], back_recv.at[1]
+                ).start()
+
+                @pl.when(holds)
+                def _():
+                    pltpu.make_async_copy(
+                        mixed.at[mine, cols_extra], new_third.at[third_part(tile)], back_recv.at[2]
+                    ).start()
+
+                @pl.when(me == BIAS_AT)
+                def _():
+                    pltpu.make_async_copy(
+                        mixed.at[mine, cols_extra], new_bias, back_recv.at[3]
+                    ).start()
+
+            @pl.when(jnp.logical_not(here))
+            def _():
+                remote(
+                    mixed.at[rows_of(j), cols_second], new_second.at[mine, :], back_send, back_recv.at[0], j
+                ).start()
+                remote(
+                    mixed.at[rows_of(j), cols_first],
+                    new_first.at[first_part(me)],
+                    back_send,
+                    back_recv.at[1],
+                    j,
+                ).start()
+
+                @pl.when(holds)
+                def _():
+                    remote(
+                        mixed.at[rows_of(j), cols_extra],
+                        new_third.at[third_part(tile)],
+                        back_extra,
+                        back_recv.at[2],
+                        j,
+                    ).start()
+
+                @pl.when(me == BIAS_AT)
+                def _():
+                    remote(
+                        mixed.at[rows_of(j), cols_extra], new_bias, back_extra, back_recv.at[3], j
+                    ).start()
+
+            return 0
+
+        lax.fori_loop(0, peers, back, 0)
+
+    def drain(ref, sem):
+        pltpu.make_async_copy(ref, ref, sem).wait()
+
+    others = pl.ds(0, (members - 1) * ROWS)
+    drain(slab.at[others, pl.ds(0, main)], send_sem)
+    at_most = 33 * ROWS
+
+    @pl.when(extra_here)
+    def _():
+        drain(slab.at[pl.ds(0, at_most - ROWS), cols_extra], send_extra)
+        drain(slab.at[others, cols_extra], back_extra)
+
+    @pl.when(jnp.logical_not(extra_here))
+    def _():
+        drain(slab.at[pl.ds(0, at_most), cols_extra], send_extra)
+
+    drain(new_second, back_recv.at[0])
+    drain(new_first, back_recv.at[1])
+    drain(new_third, back_recv.at[2])
+    drain(new_bias, back_recv.at[3])
+    drain(mixed.at[others, pl.ds(0, main)], back_send)
+
+
+def exchange(gain_tr, w_first, w_second, w_third, bias, members):
+    anywhere = pl.BlockSpec(memory_space=pl.ANY)
+    wide = w_second.shape[1] + w_first.shape[1] // 4 + LANES
+    count = members * ROWS
+    dma = pltpu.SemaphoreType.DMA
+    return pl.pallas_call(
+        functools.partial(exchange_kernel, members),
+        out_shape=[jax.ShapeDtypeStruct(a.shape, a.dtype) for a in (w_first, w_second, w_third, bias)],
+        in_specs=[pl.BlockSpec(memory_space=pltpu.VMEM)] + [anywhere] * 4,
+        out_specs=[anywhere] * 4,
+        scratch_shapes=[
+            pltpu.VMEM((count, wide), jnp.bfloat16),
+            pltpu.VMEM((count, wide), jnp.bfloat16),
+            pltpu.VMEM((512, count), jnp.bfloat16),
+            pltpu.VMEM((members, count), jnp.bfloat16),
+            pltpu.VMEM((ROWS, wide), jnp.float32),
+            dma,
+            dma,
+            dma,
+            dma,
+            dma,
+            dma,
+            dma((4,)),
+        ],
+        compiler_params=pltpu.CompilerParams(
+            collective_id=0, has_side_effects=True, vmem_limit_bytes=50 << 20
+        ),
+    )(gain_tr, w_first, w_second, w_third, bias)
 
 
 def solve_gain(amat, bmat):
@@ -22,25 +319,7 @@
     return (amat, bmat)
 
 
-def to_slabs(shards):
-    flats = [piece.reshape(1, -1) for piece in shards]
-    return (
-        lax.all_to_all(flats[0], "member", split_axis=1, concat_axis=0, tiled=True),
-        lax.all_to_all(flats[1], "member", split_axis=1, concat_axis=0, tiled=True),
-        lax.all_to_all(flats[2], "member", split_axis=1, concat_axis=0, tiled=True),
-        lax.all_to_all(flats[3], "member", split_axis=1, concat_axis=0, tiled=True),
-        lax.all_to_all(flats[4], "member", split_axis=1, concat_axis=0, tiled=True),
-    )
-
-
-def mix_slab(slab, gain_tr):
-    full = slab.astype(jnp.float32)
-    center = (full - jnp.mean(full, axis=0, keepdims=True)).astype(jnp.bfloat16)
-    return jnp.dot(gain_tr, center, preferred_element_type=jnp.float32).astype(jnp.bfloat16)
-
-
 def body(samples, w_first, b_first, w_second, b_second, w_third, observed, perturb, variance):
-    shards = (w_first, b_first, w_second, b_second, w_third)
     in_scale = samples.shape[1] ** (-0.5)
     hid_scale = w_second.shape[1] ** (-0.5)
     first = jax.nn.gelu(
@@ -73,16 +352,18 @@
     amat, bmat = lax.psum((amat, bmat), "pair")
     gain = solve_gain(amat, bmat)
     gain_tr = gain.astype(jnp.bfloat16).T
-    slabs = to_slabs(shards)
-    mixed = [mix_slab(slab, gain_tr) for slab in slabs]
-    returned = (
-        lax.all_to_all(mixed[0], "member", split_axis=0, concat_axis=1, tiled=True),
-        lax.all_to_all(mixed[1], "member", split_axis=0, concat_axis=1, tiled=True),
-        lax.all_to_all(mixed[2], "member", split_axis=0, concat_axis=1, tiled=True),
-        lax.all_to_all(mixed[3], "member", split_axis=0, concat_axis=1, tiled=True),
-        lax.all_to_all(mixed[4], "member", split_axis=0, concat_axis=1, tiled=True),
-    )
-    return tuple((back.reshape(orig.shape) for back, orig in zip(returned, shards)))
+    members = lax.axis_size("member")
+    bias = jnp.concatenate([b_first.reshape(8, -1), b_second.reshape(8, -1)], axis=0)
+    new_first, new_second, new_third, new_bias = exchange(
+        gain_tr, w_first[0], w_second[0], w_third[0].T, bias, members
+    )
+    return (
+        new_first[None],
+        new_bias[:8].reshape(b_first.shape),
+        new_second[None],
+        new_bias[8:].reshape(b_second.shape),
+        new_third.T[None],
+    )
 
 
 def solution(mesh):

time: 764 us -> 699 us (0.915)
  Pallas kernels: 0 us -> 281 us
  starting transfers between devices: 135 us -> 0.39 us
  local copies, waits for them, and re-layouts: 118 us -> 9.69 us
  other arithmetic: 140 us -> 33.2 us
  waiting for transfers between devices: 277 us -> 297 us
  matrix products: 64.9 us -> 54.7 us
    pallas_call x0 -> x1, Pallas kernels: none -> 281 us  [exchange(): pl.pallas_call(functools.partial(exchange_kernel, members), out_shape=[ja...]
    all_to_all x10 -> x0, starting transfers between devices: 134 us -> none  [the longest x1 19.7 us: to_slabs(): lax.all_to_all(flats[4], 'member', split_axis=1, concat_axis=0, tiled=True)]
    all_gather x1, waiting for transfers between devices: 0.02 us -> 124 us  [body(): lax.all_gather(pred_half, 'member', axis=0, tiled=True)]
    all_to_all x10 -> x0, waiting for transfers between devices: 96.4 us -> none  [the longest x1 70.3 us: body(): lax.all_to_all(mixed[2], 'member', split_axis=0, concat_axis=1, tiled=True)]
    unnamed x35 -> x20, local copies, waits for them, and re-layouts: 79.3 us -> 9.24 us
    all_to_all x8 -> x0, other arithmetic: 44.5 us -> none  [the longest x2 32.7 us: body(): lax.all_to_all(mixed[2], 'member', split_axis=0, concat_axis=1, tiled=True)]
    unnamed x4 -> x1, other arithmetic: 37 us -> 0.82 us
    all_to_all x9 -> x0, local copies, waits for them, and re-layouts: 28.4 us -> none  [the longest x1 19.6 us: to_slabs(): lax.all_to_all(flats[2], 'member', split_axis=1, concat_axis=0, tiled=True)]
  transfers between devices with their start and end apart: 15 -> 5, of which waited for: 9 -> 5; matrix products, arithmetic and copies ran while one was open for 30% -> 4% of each run, Pallas kernels for 0% -> 0%
where the time goes in v1:
time: 699 us; the launch traced here: 691 us
  waiting for transfers between devices  297 us (42%)
  Pallas kernels  281 us (40%)
  matrix products  54.7 us (8%)
  other arithmetic  33.2 us (5%)
  between operations  13.9 us (2%)
  local copies, waits for them, and re-layouts  9.69 us (1%)
    pallas_call x1, Pallas kernels, exchange(): pl.pallas_call(functools.partial(exchange_kernel, members), out_shape=[ja...  281 us
    all_gather x1, waiting for transfers between devices, body(): lax.all_gather(pred_half, 'member', axis=0, tiled=True)  124 us
    all_gather x1, waiting for transfers between devices, body(): lax.all_gather(res_half, 'member', axis=0, tiled=True)  96.3 us
    psum x1, waiting for transfers between devices, body(): pred = lax.psum(partial_out, 'pair')  30.1 us
    psum x1, waiting for transfers between devices, body(): amat, bmat = lax.psum((amat, bmat), 'pair')  27.7 us
    dot_general x1, matrix products, moments(): bmat = jnp.dot(scaled, allres.T, precision=lax.Precision.HIGHEST)  21.7 us
    dot_general x1, matrix products, moments(): amat = jnp.dot(scaled, devpred.T, precision=lax.Precision.HIGHEST)  21.7 us
    all_gather x1, waiting for transfers between devices, body(): lax.all_gather(first, 'pair', axis=1, tiled=True)  18.6 us
  transfers between devices with their start and end apart: 5, of which 5 were waited for; matrix products, arithmetic and copies ran while one was open for 4% of the time, Pallas kernels for 0%

profile of v1, /device:TPU:30, one launch (start us, length us, event | category | flops | bytes accessed | tf_op | source)
XLA Modules:
  0.0 690.5 jit_solution(220004657682223326)
XLA Ops:
  7.2 0.8 fusion.49
  8.3 3.5 fusion.17
  11.8 18.6 %all-gather.6.cloned.1.call-done = bf16[512,2048]{1,0:T(8,128)(2,1)} async-done(((bf16[512,1024]{1,0:T(8,128)(2,1)}), bf16[512,2048]{1,0:T(8,128)(2,1)}) %all-gather.6.cloned.1.call-update) | async-done | bytes 2097168 | tf_op jit(solution)/shard_map/all_gather | solution.py:332
  30.5 6.5 fusion.27
  37.0 30.1 %all-reduce.4.cloned.1.call-done = f32[512,64]{0,1:T(8,128)} async-done(((f32[512,64]{0,1:T(8,128)}), f32[512,64]{0,1:T(8,128)}) %all-reduce.4.cloned.1.call-update) | async-done | bytes 131088 | tf_op jit(solution)/shard_map/psum | solution.py:340
  67.1 0.9 constant_dynamic-slice_fusion
  68.1 0.8 reshape.53
  69.1 0.8 reshape.55
  70.3 124.3 %all-gather.8.cloned.1.call-done = f32[128,1,16384]{2,1,0:T(1,128)} async-done(((f32[1,1,16384]{2,1,0:T(1,128)}), f32[128,1,16384]{2,1,0:T(1,128)}) %all-gather.8.cloned.1.call-update) | async-done | bytes 8388624 | tf_op jit(solution)/shard_map/all_gather | solution.py:348
  194.6 6.9 reduce_sum.9
  201.5 21.7 %fusion.4 = f32[128,128]{1,0:T(8,128)} fusion(f32[128,1,16384]{2,1,0:T(1,128)} %all-gather.8.cloned.1.call-done, f32[16384]{0:T(1024)S(1)} %div.26, f32[16384]{0:T(1024)S(1)} %broadcast_multiply_fusion), kind=kOutput, calls=%fused_computation.5 | convolution fusion | flops 3227516928 | bytes 8585216 | tf_op jit(solution)/shard_map/dot_general | solution.py:317
  223.2 96.3 %all-gather.10.cloned.1.call-done = f32[128,1,16384]{2,1,0:T(1,128)} async-done(((f32[1,1,16384]{2,1,0:T(1,128)}), f32[128,1,16384]{2,1,0:T(1,128)}) %all-gather.10.cloned.1.call-update) | async-done | bytes 8388624 | tf_op jit(solution)/shard_map/all_gather | solution.py:349
  319.4 21.7 %fusion = f32[128,128]{1,0:T(8,128)} fusion(f32[128,1,16384]{2,1,0:T(1,128)} %all-gather.10.cloned.1.call-done, f32[128,1,16384]{2,1,0:T(1,128)} %all-gather.8.cloned.1.call-done, f32[16384]{0:T(1024)S(1)} %div.26, f32[16384]{0:T(1024)S(1)} %broadcast_multiply_fusion), kind=kOutput, calls=%fused_computation | convolution fusion | flops 3225419776 | bytes 16973824 | tf_op jit(solution)/shard_map/dot_general | solution.py:318
  341.2 27.7 %all-reduce.6.cloned.1.call-done = (f32[128,128]{1,0:T(8,128)}, f32[128,128]{1,0:T(8,128)}) async-done(((f32[128,128]{1,0:T(8,128)}, f32[128,128]{1,0:T(8,128)}), (f32[128,128]{1,0:T(8,128)}, f32[128,128]{1,0:T(8,128)})) %all-reduce.6.cloned.1.call-update) | async-done | bytes 131088 | tf_op jit(solution)/shard_map/psum | solution.py:352
  368.9 0.9 select_add_fusion
  369.8 0.9 fusion.40
  370.7 11.7 %cholesky.16 = f32[128,128]{1,0:T(8,128)S(1)} custom-call(f32[128,128]{1,0:T(8,128)S(1)} %fusion.40), custom_call_target="Cholesky" | custom-call | tf_op jit(solution)/shard_map/jit(cholesky)/cholesky | solution.py:307
  383.1 0.7 fusion.35
  383.7 9.8 %custom-call.8 = f32[1,128,128]{1,2,0:T(8,128)S(1)} custom-call(f32[1,128,128]{2,1,0:T(8,128)S(1)} %fusion.35), custom_call_target="InvertDiagBlocksLowerTriangular" | custom-call | tf_op jit(solution)/shard_map/triangular_solve | solution.py:311
  393.6 1.1 fusion.38
  395.0 281.5 %shard_map.128 = (bf16[512,1024]{1,0:T(8,128)(2,1)S(1)}, bf16[2048,1024]{1,0:T(8,128)(2,1)}, bf16[64,1024]{1,0:T(8,128)(2,1)S(1)}, bf16[16,128]{1,0:T(8,128)(2,1)S(1)}) custom-call(bf16[128,128]{1,0:T(8,128)(2,1)S(1)} %convolution_convert_fusion.gain_tr, bf16[512,1024]{1,0:T(8,128)(2,1)S(1)} %bitcast.61, bf16[2048,1024]{1,0:T(8,128)(2,1)} %bitcast.64, ...), custom_call_target="tpu_custom_call" | custom-call | tf_op jit(solution)/shard_map/pallas_call | solution.py:279
  677.7 1.0 copy.48
  678.7 4.6 copy.49
  683.3 0.7 copy.50
  (35 shorter events, 3.3 us)
Async XLA Ops:
  7.2 1.1 copy-start
  7.2 23.3 %all-gather.6.cloned.1.call-start = ((), (), s32[]{:S(2)}) async-start(), calls=%async_computation | async-start | bytes 3145728 | tf_op jit(solution)/shard_map/all_gather | solution.py:332
  8.3 22.2 %copy-start.2 = (bf16[1,1024,64]{1,2,0:T(8,128)(2,1)S(1)}, bf16[1,1024,64]{1,2,0:T(8,128)(2,1)}, u32[]{:S(2)}) copy-start(bf16[1,1024,64]{1,2,0:T(8,128)(2,1)} %param.14) | copy-start | bytes 393220
  11.8 55.4 %all-reduce.4.cloned.1.call-start = ((), (), s32[]{:S(2)}) async-start(), calls=%async_computation.1 | async-start | bytes 262144 | tf_op jit(solution)/shard_map/psum | solution.py:340
  30.5 36.7 %copy-start.3 = (f32[512,64]{0,1:T(8,128)S(1)}, f32[512,64]{0,1:T(8,128)}, u32[]{:S(2)}) copy-start(f32[512,64]{0,1:T(8,128)} %param.17) | copy-start | bytes 393220
  30.5 36.7 %copy-start.4 = (f32[1,512,64]{1,2,0:T(8,128)S(1)}, f32[1,512,64]{1,2,0:T(8,128)}, u32[]{:S(2)}) copy-start(f32[1,512,64]{1,2,0:T(8,128)} %param.16) | copy-start | bytes 393220
  30.5 36.7 %copy-start.5 = (f32[512,64]{0,1:T(8,128)S(1)}, f32[512,64]{0,1:T(8,128)}, u32[]{:S(2)}) copy-start(f32[512,64]{0,1:T(8,128)} %param.15) | copy-start | bytes 393220
  37.0 157.6 %all-gather.8.cloned.1.call-start = ((), (), s32[]{:S(2)}) async-start(), calls=%async_computation.2 | async-start | bytes 8454144 | tf_op jit(solution)/shard_map/all_gather | solution.py:348
  68.9 250.5 %all-gather.10.cloned.1.call-start = ((), (), s32[]{:S(2)}) async-start(), calls=%async_computation.3 | async-start | bytes 8454144 | tf_op jit(solution)/shard_map/all_gather | solution.py:349
  69.8 299.0 %all-reduce.6.cloned.1.call-start = ((), (), s32[]{:S(2)}) async-start(), calls=%async_computation.4 | async-start | bytes 262144 | tf_op jit(solution)/shard_map/psum | solution.py:352
  223.2 171.8 %copy-start.1 = (bf16[1,512,1024]{2,1,0:T(8,128)(2,1)S(1)}, bf16[1,512,1024]{2,1,0:T(8,128)(2,1)}, u32[]{:S(2)}) copy-start(bf16[1,512,1024]{2,1,0:T(8,128)(2,1)} %param.10) | copy-start | bytes 3145732
Sparse Core Ops, SparseCore 0:
  11.9 18.5 all-gather.5
  37.1 29.9 all-reduce.3
  71.3 123.2 all-gather.7
  198.6 120.7 all-gather.9
  341.3 27.5 all-reduce.5

commit v2 on v0

v2 whole, which is shorter than its diff:
```python
import functools

import jax
import jax.numpy as jnp
from jax import lax
from jax.experimental import pallas as pl
from jax.experimental.pallas import tpu as pltpu
from jax.sharding import PartitionSpec as P

MESH = pl.DeviceIdType.MESH
ROWS = 16
LANES = 128
THIRDS = 32
BIAS_AT = 4
PACE = 8
WINDOW = 4
GROUP = 512
LAST = (((1,), (1,)), ((), ()))


def peer_at(me, i):
    y, z, x = me // 32, lax.rem(me // 4, 8), lax.rem(me, 4)
    dz, dx, dy = i & 7, (i >> 3) & 3, i >> 5
    return ((y + dy) & 3) * 32 + ((z + dz) & 7) * 4 + ((x + dx) & 3)


def holder(e):
    y, x = e // 8, lax.rem(e // 2, 4)
    return y * 32 + (lax.rem(x + y, 4) + 4 * lax.rem(e, 2)) * 4 + x


def own_tile(me):
    y, z, x = me // 32, lax.rem(me // 4, 8), lax.rem(me, 4)
    return lax.rem(z, 4) == lax.rem(x + y, 4), y * 8 + x * 2 + z // 4


def kernel(
    members,
    in_scale,
    hid_scale,
    samples,
    w_first,
    b_first,
    w_second,
    b_second,
    w_third_hbm,
    observed,
    perturb,
    variance,
    new_first,
    new_bfirst,
    new_second,
    new_bsecond,
    new_third,
    slab,
    mixed,
    weights,
    spread,
    avg,
    inputs,
    first_w,
    second_w,
    third_w,
    act_own,
    act_peer,
    second,
    out_t,
    out_peer,
    outgoing,
    columns,
    moments,
    partials,
    row,
    row_peer,
    system,
    spare_a,
    spare_b,
    spare_c,
    bias_wide,
    bias,
    bias_back,
    load_sem,
    send_sem,
    recv_sem,
    send_extra,
    recv_extra,
    pair_send,
    pair_recv,
    small_send,
    small_recv,
    back_send,
    back_extra,
    back_recv,
):
    me, core = lax.axis_index("member"), lax.axis_index("pair")
    other = 1 - core
    spares = (spare_a, spare_b, spare_c)
    wide = w_second.shape[1]
    narrow = w_first.shape[1] // 4
    main = wide + narrow
    count = members * ROWS
    holds, tile = own_tile(me)
    extra_here = jnp.logical_or(holds, me == BIAS_AT)

    def rows_of(p):
        return pl.ds(pl.multiple_of(p * ROWS, ROWS), ROWS)

    def first_part(p):
        return (
            pl.ds(pl.multiple_of((p // 4) * ROWS, ROWS), ROWS),
            pl.ds(pl.multiple_of(lax.rem(p, 4) * narrow, narrow), narrow),
        )

    def third_part(e):
        return (
            pl.ds(pl.multiple_of((e // 8) * ROWS, ROWS), ROWS),
            pl.ds(pl.multiple_of(lax.rem(e, 8) * LANES, LANES), LANES),
        )

    def remote(src, dst, send, recv, peer, to_core=None):
        return pltpu.make_async_remote_copy(
            src_ref=src,
            dst_ref=dst,
            send_sem=send,
            recv_sem=recv,
            device_id=(peer, core if to_core is None else to_core),
            device_id_type=MESH,
        )

    def drain(ref, sem):
        pltpu.make_async_copy(ref, ref, sem).wait()

    mine = rows_of(me)
    cols_second, cols_first, cols_extra = pl.ds(0, wide), pl.ds(wide, narrow), pl.ds(main, LANES)

    barrier = pltpu.get_barrier_semaphore()

    def greet(i, _):
        pl.semaphore_signal(
            barrier, inc=1, device_id=(peer_at(me, i), core), device_id_type=MESH
        )
        return 0

    lax.fori_loop(1, members, greet, 0)
    pl.semaphore_signal(barrier, inc=1, device_id=(me, other), device_id_type=MESH)

    loads = [
        pltpu.make_async_copy(samples, inputs, load_sem.at[0]),
        pltpu.make_async_copy(w_first, first_w, load_sem.at[1]),
        pltpu.make_async_copy(w_second, second_w, load_sem.at[2]),
        pltpu.make_async_copy(w_third_hbm, third_w, load_sem.at[3]),
    ]
    for load in loads:
        load.start()

    def bias_rows(i, ref, at):
        bias_wide[at + i : at + i + 1, :] = ref[:, i * LANES : (i + 1) * LANES].astype(jnp.float32)

    for i in range(8):
        bias_rows(i, b_first, 0)
        bias_rows(i, b_second, 8)
    bias[...] = bias_wide[...].astype(jnp.bfloat16)

    pl.semaphore_wait(barrier, members)

    def push(i, g):
        p = peer_at(me, i)
        remote(
            w_second.at[rows_of(p), :], slab.at[mine, cols_second], send_sem.at[g], recv_sem, p
        ).start()
        remote(
            w_first.at[first_part(p)], slab.at[mine, cols_first], send_sem.at[g], recv_sem, p
        ).start()

    def push_group(g):
        def one(i, _):
            push(i, g)
            return 0

        lax.fori_loop(max(1, g * PACE), (g + 1) * PACE, one, 0)

    def sent_group(g):
        n = (PACE if g else PACE - 1) * ROWS
        drain(slab.at[pl.ds(0, n), pl.ds(0, main)], send_sem.at[g])

    groups = members // PACE
    state = [0]

    def pump(n):
        for _ in range(n):
            g = state[0]
            if g >= groups:
                return
            if g >= WINDOW:
                sent_group(g - WINDOW)
            push_group(g)
            state[0] = g + 1

    def push_extra(e, _):
        p = holder(e)
        here = p == me

        @pl.when(here)
        def _():
            pltpu.make_async_copy(
                w_third_hbm.at[third_part(e)], slab.at[mine, cols_extra], recv_extra
            ).start()

        @pl.when(jnp.logical_not(here))
        def _():
            remote(
                w_third_hbm.at[third_part(e)], slab.at[mine, cols_extra], send_extra, recv_extra, p
            ).start()

        return 0

    pltpu.make_async_copy(w_second.at[mine, :], slab.at[mine, cols_second], recv_sem).start()
    pltpu.make_async_copy(w_first.at[first_part(me)], slab.at[mine, cols_first], recv_sem).start()
    pump(WINDOW)

    loads[0].wait()
    loads[1].wait()

    @pl.loop(0, wide // 256)
    def _(n):
        c = pl.ds(pl.multiple_of(n * 256, 256), 256)
        h = jnp.dot(inputs[...], first_w[:, c], preferred_element_type=jnp.float32) * in_scale
        h = h + b_first[:, c].astype(jnp.float32)
        act_own[:, c] = jax.nn.gelu(h, approximate=True).astype(jnp.bfloat16)

    to_pair = remote(act_own, act_peer, pair_send.at[0], pair_recv.at[0], me, other)
    to_pair.start()
    pump(1)
    loads[2].wait()
    loads[3].wait()
    to_pair.wait()
    half = second_w.shape[0] // 2
    own_rows = pl.ds(pl.multiple_of(core * half, half), half)
    peer_rows = pl.ds(pl.multiple_of(other * half, half), half)

    @pl.loop(0, wide // 256)
    def _(n):
        c = pl.ds(pl.multiple_of(n * 256, 256), 256)
        h = jnp.dot(act_own[...], second_w[own_rows, c], preferred_element_type=jnp.float32)
        h = h + jnp.dot(act_peer[...], second_w[peer_rows, c], preferred_element_type=jnp.float32)
        h = h * hid_scale + b_second[:, c].astype(jnp.float32)
        second[:, c] = jax.nn.gelu(h, approximate=True).astype(jnp.bfloat16)

    out_t[...] = (
        lax.dot_general(third_w[...], second[...], LAST, preferred_element_type=jnp.float32)
        * hid_scale
    )
    part = out_t.shape[1] // 2
    own_cols = pl.ds(pl.multiple_of(core * part, part), part)
    peer_cols = pl.ds(pl.multiple_of(other * part, part), part)
    to_pair = remote(out_t.at[:, peer_cols], out_peer, pair_send.at[1], pair_recv.at[1], me, other)
    to_pair.start()
    pump(1)
    to_pair.wait()
    pred = out_t[:, own_cols] + out_peer[...]
    resid = observed[:, own_cols] + jnp.sqrt(variance[:, own_cols]) * perturb[:, own_cols] - pred
    tall = pred.shape[0]
    for k in range(2):
        outgoing[k * tall : (k + 1) * tall, 0:LANES] = pred[:, k * LANES : (k + 1) * LANES]
        outgoing[k * tall : (k + 1) * tall, LANES:] = resid[:, k * LANES : (k + 1) * LANES]

    def line(ref, p):
        return ref.at[pl.ds(p, 1), :]

    def scatter_rows(src, dst, k, whole):
        def one(i, _):
            p = peer_at(me, i)
            remote(
                src if whole else line(src, p), line(dst, me), small_send.at[k], small_recv.at[k], p
            ).start()
            return 0

        lax.fori_loop(1, members, one, 0)
        own = src if whole else line(src, me)
        pltpu.make_async_copy(own, line(dst, me), small_recv.at[k]).start()
        pltpu.make_async_copy(own, spares[k], small_send.at[k]).start()

    scatter_rows(outgoing, columns, 0, False)
    pump(1)
    drain(columns, small_recv.at[0])
    pred_all, res_all = columns[:, 0:LANES], columns[:, LANES:]
    dev = pred_all - jnp.mean(pred_all, axis=0, keepdims=True)
    var_at = core * part + (me // tall) * LANES
    var_rows = variance[:, pl.ds(pl.multiple_of(var_at, LANES), LANES)]
    its_row = lax.broadcasted_iota(jnp.int32, (tall, LANES), 0) == lax.rem(me, tall)
    var_here = jnp.sum(jnp.where(its_row, var_rows, 0.0), axis=0, keepdims=True)
    scaled = dev / var_here
    exact = lax.Precision.HIGHEST
    moments[:, 0:LANES] = lax.dot_general(
        scaled, dev, LAST, precision=exact, preferred_element_type=jnp.float32
    )
    moments[:, LANES:] = lax.dot_general(
        scaled, res_all, LAST, precision=exact, preferred_element_type=jnp.float32
    )

    scatter_rows(moments, partials, 1, False)
    pump(1)
    drain(partials, small_recv.at[1])
    row[...] = jnp.sum(partials[...], axis=0, keepdims=True)
    to_pair = remote(row, row_peer, pair_send.at[2], pair_recv.at[2], me, other)
    to_pair.start()
    to_pair.wait()
    row[...] = row[...] + row_peer[...]
    scatter_rows(row, system, 2, True)
    pump(1)
    lax.fori_loop(0, THIRDS, push_extra, 0)

    @pl.when(me == BIAS_AT)
    def _():
        pltpu.make_async_copy(bias, slab.at[mine, cols_extra], recv_extra).start()

    @pl.when(me != BIAS_AT)
    def _():
        remote(bias, slab.at[mine, cols_extra], send_extra, recv_extra, BIAS_AT).start()

    at = lax.broadcasted_iota(jnp.int32, (members, count), 1) // ROWS
    who = lax.broadcasted_iota(jnp.int32, (members, count), 0)
    spread[...] = jnp.where(at == who, 1.0, 0.0).astype(jnp.bfloat16)
    drain(system, small_recv.at[2])

    d0 = lax.broadcasted_iota(jnp.int32, (members, members), 0)
    d1 = lax.broadcasted_iota(jnp.int32, (members, members), 1)
    system[:, 0:members] = system[:, 0:members] + jnp.where(d0 == d1, float(members), 0.0)
    lane = lax.broadcasted_iota(jnp.int32, (1, 2 * members), 1)

    def eliminate(i, _):
        now = system[...]
        top = system[pl.ds(i, 1), :]
        col = jnp.sum(jnp.where(lane == i, now, 0.0), axis=1, keepdims=True)
        pivot = jnp.sum(jnp.where(lane == i, top, 0.0), axis=1, keepdims=True)
        top = top / pivot
        system[...] = now - col * top
        system[pl.ds(i, 1), :] = top
        return 0

    for k in range(8):
        step = members // 8
        lax.fori_loop(k * step, (k + 1) * step, eliminate, 0)
        pump(1)
    pump(groups)
    gain = system[:, members:].astype(jnp.bfloat16)
    spread_gain = gain

    peers = GROUP // ROWS

    def weigh(g):
        ir = lax.broadcasted_iota(jnp.int32, (GROUP, members), 0) // ROWS + g * peers
        jj = lax.broadcasted_iota(jnp.int32, (GROUP, members), 1)
        pick = jnp.where(peer_at(me, ir) == jj, 1.0, 0.0).astype(jnp.bfloat16)
        rep = lax.dot_general(pick, spread_gain, LAST, preferred_element_type=jnp.float32)
        rep16 = rep.astype(jnp.bfloat16)

        @pl.loop(0, count // 512)
        def _(q):
            c = pl.ds(pl.multiple_of(q * 512, 512), 512)
            full = jnp.dot(rep16, spread[:, c], preferred_element_type=jnp.float32)
            r0 = lax.broadcasted_iota(jnp.int32, (GROUP, 512), 0) % ROWS
            r1 = lax.broadcasted_iota(jnp.int32, (GROUP, 512), 1) % ROWS
            weights[pl.ds(0, GROUP), c] = jnp.where(r0 == r1, full, 0.0).astype(jnp.bfloat16)

        return jnp.sum(rep, axis=1, keepdims=True)

    tr = lax.broadcasted_iota(jnp.int32, (ROWS, count), 1) % ROWS
    tw = lax.broadcasted_iota(jnp.int32, (ROWS, count), 0)
    weights[pl.ds(GROUP, ROWS), :] = jnp.where(tr == tw, 1.0, 0.0).astype(jnp.bfloat16)

    def mix(g, weight_sum, c, width):
        out_rows = pl.ds(pl.multiple_of(g * GROUP, GROUP), GROUP)
        if isinstance(g, int):
            acc = jnp.dot(weights[...], slab[:, c], preferred_element_type=jnp.float32)
            avg[:, c] = acc[GROUP:, :] * (1.0 / members)
            acc = acc[:GROUP, :]
        else:
            acc = jnp.dot(
                weights[pl.ds(0, GROUP), :], slab[:, c], preferred_element_type=jnp.float32
            )
        means = jnp.broadcast_to(avg[:, c][None], (peers, ROWS, width)).reshape(GROUP, width)
        mixed[out_rows, c] = (acc - weight_sum * means).astype(jnp.bfloat16)

    def mix_all(g, weight_sum):
        @pl.loop(0, main // 256)
        def _(n):
            mix(g, weight_sum, pl.ds(pl.multiple_of(n * 256, 256), 256), 256)

        @pl.when(extra_here)
        def _():
            mix(g, weight_sum, cols_extra, LANES)

    def send_back(i, _):
        j = peer_at(me, i)
        remote(
            mixed.at[rows_of(i), cols_second], new_second.at[mine, :], back_send, back_recv.at[0], j
        ).start()
        remote(
            mixed.at[rows_of(i), cols_first],
            new_first.at[first_part(me)],
            back_send,
            back_recv.at[1],
            j,
        ).start()

        @pl.when(holds)
        def _():
            remote(
                mixed.at[rows_of(i), cols_extra],
                new_third.at[third_part(tile)],
                back_extra,
                back_recv.at[2],
                j,
            ).start()

        @pl.when(me == BIAS_AT)
        def _():
            remote(
                mixed.at[rows_of(i), cols_extra], bias_back, back_extra, back_recv.at[3], j
            ).start()

        return 0

    def keep_own():
        here = pl.ds(0, ROWS)
        pltpu.make_async_copy(
            mixed.at[here, cols_second], new_second.at[mine, :], back_recv.at[0]
        ).start()
        pltpu.make_async_copy(
            mixed.at[here, cols_first], new_first.at[first_part(me)], back_recv.at[1]
        ).start()

        @pl.when(holds)
        def _():
            pltpu.make_async_copy(
                mixed.at[here, cols_extra], new_third.at[third_part(tile)], back_recv.at[2]
            ).start()

        @pl.when(me == BIAS_AT)
        def _():
            pltpu.make_async_copy(mixed.at[here, cols_extra], bias_back, back_recv.at[3]).start()

    weight_sum = weigh(0)
    drain(slab.at[:, pl.ds(0, main)], recv_sem)

    @pl.when(extra_here)
    def _():
        drain(slab.at[:, cols_extra], recv_extra)

    mix_all(0, weight_sum)
    keep_own()
    lax.fori_loop(1, peers, send_back, 0)

    @pl.loop(1, members // peers)
    def _(g):
        mix_all(g, weigh(g))
        lax.fori_loop(g * peers, (g + 1) * peers, send_back, 0)

    others = pl.ds(0, (members - 1) * ROWS)
    for g in range(groups - WINDOW, groups):
        sent_group(g)
    for k in range(3):
        drain(outgoing, small_send.at[k])

    @pl.when(extra_here)
    def _():
        drain(slab.at[pl.ds(0, THIRDS * ROWS), cols_extra], send_extra)
        drain(slab.at[others, cols_extra], back_extra)

    @pl.when(jnp.logical_not(extra_here))
    def _():
        drain(slab.at[pl.ds(0, (THIRDS + 1) * ROWS), cols_extra], send_extra)

    drain(bias_back, back_recv.at[3])
    bias_wide[...] = bias_back[...].astype(jnp.float32)
    for i in range(8):
        c = slice(i * LANES, (i + 1) * LANES)
        new_bfirst[:, c] = bias_wide[i : i + 1, :].astype(jnp.bfloat16)
        new_bsecond[:, c] = bias_wide[8 + i : 9 + i, :].astype(jnp.bfloat16)
    drain(new_first, back_recv.at[1])
    drain(new_third, back_recv.at[2])
    drain(new_second, back_recv.at[0])
    drain(mixed.at[others, pl.ds(0, main)], back_send)


def body(samples, w_first, b_first, w_second, b_second, w_third, observed, perturb, variance):
    members = lax.axis_size("member")
    in_scale = samples.shape[1] ** (-0.5)
    hid_scale = w_second.shape[1] ** (-0.5)
    first_w, second_w, third_w = w_first[0], w_second[0], w_third[0].T
    count = members * ROWS
    wide = second_w.shape[1] + first_w.shape[1] // 4 + LANES
    batch, hidden, outs = samples.shape[0], second_w.shape[1], third_w.shape[0]
    anywhere = pl.BlockSpec(memory_space=pl.ANY)
    onchip = pl.BlockSpec(memory_space=pltpu.VMEM)
    dma = pltpu.SemaphoreType.DMA
    low, full = jnp.bfloat16, jnp.float32
    shapes = (first_w, b_first, second_w, b_second, third_w)
    new_first, new_bfirst, new_second, new_bsecond, new_third = pl.pallas_call(
        functools.partial(kernel, members, in_scale, hid_scale),
        out_shape=[jax.ShapeDtypeStruct(a.shape, a.dtype) for a in shapes],
        in_specs=[anywhere, anywhere, onchip, anywhere, onchip, anywhere, onchip, onchip, onchip],
        out_specs=[anywhere, onchip, anywhere, onchip, anywhere],
        scratch_shapes=[
            pltpu.VMEM((count, wide), low),
            pltpu.VMEM((count, wide), low),
            pltpu.VMEM((GROUP + ROWS, count), low),
            pltpu.VMEM((members, count), low),
            pltpu.VMEM((ROWS, wide), full),
            pltpu.VMEM(samples.shape, low),
            pltpu.VMEM(first_w.shape, low),
            pltpu.VMEM(second_w.shape, low),
            pltpu.VMEM(third_w.shape, low),
            pltpu.VMEM((batch, hidden), low),
            pltpu.VMEM((batch, hidden), low),
            pltpu.VMEM((batch, hidden), low),
            pltpu.VMEM((outs, batch), full),
            pltpu.VMEM((outs, batch // 2), full),
            pltpu.VMEM((members, 2 * LANES), full),
            pltpu.VMEM((members, 2 * LANES), full),
            pltpu.VMEM((members, 2 * LANES), full),
            pltpu.VMEM((members, 2 * LANES), full),
            pltpu.VMEM((1, 2 * LANES), full),
            pltpu.VMEM((1, 2 * LANES), full),
            pltpu.VMEM((members, 2 * LANES), full),
            pltpu.VMEM((1, 2 * LANES), full),
            pltpu.VMEM((1, 2 * LANES), full),
            pltpu.VMEM((1, 2 * LANES), full),
            pltpu.VMEM((ROWS, LANES), full),
            pltpu.VMEM((ROWS, LANES), low),
            pltpu.VMEM((ROWS, LANES), low),
            dma((4,)),
            dma((members // PACE,)),
            dma,
            dma,
            dma,
            dma((3,)),
            dma((3,)),
            dma((3,)),
            dma((3,)),
            dma,
            dma,
            dma((4,)),
        ],
        compiler_params=pltpu.CompilerParams(
            collective_id=0, has_side_effects=True, vmem_limit_bytes=50 << 20
        ),
    )(
        samples,
        first_w,
        b_first,
        second_w,
        b_second,
        third_w,
        observed.T,
        perturb[0].T,
        variance.T,
    )
    return (new_first[None], new_bfirst, new_second[None], new_bsecond, new_third.T[None])


def solution(mesh):
    in_specs = (
        P(),
        P("member", None, "pair"),
        P("member", "pair"),
        P("member", None, "pair"),
        P("member", "pair"),
        P("member", "pair", None),
        P(),
        P("member", None, None),
        P(),
    )
    out_specs = (
        P("member", None, "pair"),
        P("member", "pair"),
        P("member", None, "pair"),
        P("member", "pair"),
        P("member", "pair", None),
    )
    return jax.shard_map(body, mesh=mesh, in_specs=in_specs, out_specs=out_specs, check_vma=False)
```

time: 764 us -> 292 us (0.38); the launches traced: 750 us -> 288 us
  waiting for transfers between devices: 277 us -> 0 us
  Pallas kernels: 0 us -> 273 us
  other arithmetic: 140 us -> 0 us
  starting transfers between devices: 135 us -> 0 us
  local copies, waits for them, and re-layouts: 118 us -> 14.7 us
  matrix products: 64.9 us -> 0 us
  between operations: 14.3 us -> 0.66 us
    pallas_call x0 -> x1, Pallas kernels: none -> 273 us  [body(): pl.pallas_call(functools.partial(kernel, members, in_scale, hid_scale), o...]
    all_to_all x10 -> x0, starting transfers between devices: 134 us -> none  [the longest x1 19.7 us: to_slabs(): lax.all_to_all(flats[4], 'member', split_axis=1, concat_axis=0, tiled=True)]
    all_gather x3 -> x0, waiting for transfers between devices: 126 us -> none  [the longest x1 107 us: body(): lax.all_gather(res_half, 'member', axis=0, tiled=True)]
    all_to_all x10 -> x0, waiting for transfers between devices: 96.4 us -> none  [the longest x1 70.3 us: body(): lax.all_to_all(mixed[2], 'member', split_axis=0, concat_axis=1, tiled=True)]
    unnamed x35 -> x21, local copies, waits for them, and re-layouts: 79.3 us -> 14.7 us
    dot_general x9 -> x0, matrix products: 63.5 us -> none  [the longest x1 21.6 us: moments(): bmat = jnp.dot(scaled, allres.T, precision=lax.Precision.HIGHEST)]
    psum x2 -> x0, waiting for transfers between devices: 55.2 us -> none  [the longest x1 30.1 us: body(): pred = lax.psum(partial_out, 'pair')]
    all_to_all x8 -> x0, other arithmetic: 44.5 us -> none  [the longest x2 32.7 us: body(): lax.all_to_all(mixed[2], 'member', split_axis=0, concat_axis=1, tiled=True)]
  transfers between devices with their start and end apart: 15 -> 0, of which waited for: 9 -> 0; matrix products, arithmetic and copies ran while one was open for 30% -> 0% of each run, Pallas kernels for 0% -> 0%
where the time goes in v2:
time: 292 us; the launch traced here: 288 us
  Pallas kernels  273 us (93%)
  local copies, waits for them, and re-layouts  14.7 us (5%)
    pallas_call x1, Pallas kernels, body(): pl.pallas_call(functools.partial(kernel, members, in_scale, hid_scale), o...  273 us
    unnamed x21, local copies, waits for them, and re-layouts  14.7 us

profile of v2, /device:TPU:30, one launch (start us, length us, event | category | flops | bytes accessed | tf_op | source)
XLA Modules:
  0.0 287.9 jit_solution(15197812049406145582)
XLA Ops:
  0.6 0.0 copy-start
  0.6 1.2 copy-done
  1.9 0.0 copy-start.1
  1.9 1.0 copy-done.1
  2.9 0.0 copy-start.2
  2.9 0.9 copy-done.2
  3.8 0.0 copy-start.3
  3.8 0.9 copy-done.3
  4.7 0.0 copy-start.4
  4.7 0.9 copy-done.4
  5.6 0.0 copy-start.5
  5.6 0.9 copy-done.5
  6.5 0.0 copy-start.6
  6.5 0.7 copy-done.6
  7.2 0.0 copy-start.7
  7.2 0.7 copy-done.7
  7.9 272.6 %shard_map.128 = (bf16[512,1024]{1,0:T(8,128)(2,1)S(1)}, bf16[1,1024]{1,0:T(2,128)(2,1)S(1)}, bf16[2048,1024]{1,0:T(8,128)(2,1)}, bf16[1,1024]{1,0:T(2,128)(2,1)S(1)}, bf16[64,1024]{1,0:T(8,128)(2,1)S(1)}) custom-call(bf16[512,512]{1,0:T(8,128)(2,1)S(1)} %copy-done.1, bf16[512,1024]{1,0:T(8,128)(2,1)S(1)} %bitcast.16, bf16[1,1024]{1,0:T(2,128)(2,1)S(1)} %copy-done.6, ...), custom_call_target="tpu_custom_call" | custom-call | tf_op jit(solution)/shard_map/pallas_call | solution.py:500
  280.5 1.0 copy.19
  281.4 0.6 copy.20
  282.0 4.6 %copy.21 = bf16[1,2048,1024]{2,1,0:T(8,128)(2,1)} copy(bf16[1,2048,1024]{2,1,0:T(8,128)(2,1)} %bitcast.23) | data formatting | bytes 8388608
  286.7 0.6 copy.22
  287.3 0.7 copy.23
Async XLA Ops:
  0.6 1.2 copy-start
  1.9 1.0 copy-start.1
  2.9 0.9 copy-start.2
  3.8 0.9 copy-start.3
  4.7 0.9 copy-start.4
  5.6 0.9 copy-start.5
  6.5 0.7 copy-start.6
  7.2 0.7 copy-start.7

commit v3 on v2

v3 whole, which is shorter than its diff:
```python
import functools

import jax
import jax.numpy as jnp
from jax import lax
from jax.experimental import pallas as pl
from jax.experimental.pallas import tpu as pltpu
from jax.sharding import PartitionSpec as P

MESH = pl.DeviceIdType.MESH
ROWS = 16
LANES = 128
THIRDS = 32
BIAS_AT = 4
PACE = 8
PLAN = (6, 2, 0, 2, 2, 0)
GROUP = 256
LAST = (((1,), (1,)), ((), ()))


def peer_at(me, i):
    y, z, x = me // 32, lax.rem(me // 4, 8), lax.rem(me, 4)
    dz, dx, dy = i & 7, (i >> 3) & 3, i >> 5
    return ((y + dy) & 3) * 32 + ((z + dz) & 7) * 4 + ((x + dx) & 3)


def holder(e):
    y, x = e // 8, lax.rem(e // 2, 4)
    return y * 32 + (lax.rem(x + y, 4) + 4 * lax.rem(e, 2)) * 4 + x


def own_tile(me):
    y, z, x = me // 32, lax.rem(me // 4, 8), lax.rem(me, 4)
    return lax.rem(z, 4) == lax.rem(x + y, 4), y * 8 + x * 2 + z // 4


def kernel(
    members,
    in_scale,
    hid_scale,
    samples,
    w_first,
    b_first_hbm,
    w_second,
    b_second_hbm,
    w_third_hbm,
    observed_hbm,
    perturb_hbm,
    variance_hbm,
    new_first,
    new_bfirst,
    new_second,
    new_bsecond,
    new_third,
    slab,
    mixed,
    weights,
    weight_sums,
    spread,
    avg,
    inputs,
    first_w,
    second_w,
    third_w,
    b_first,
    b_second,
    observed,
    perturb,
    variance,
    act_own,
    act_peer,
    second,
    out_t,
    out_peer,
    outgoing,
    columns,
    moments,
    partials,
    row,
    row_peer,
    system,
    spare_a,
    spare_b,
    spare_c,
    bias_wide,
    bias,
    bias_back,
    load_sem,
    send_sem,
    recv_sem,
    send_extra,
    recv_extra,
    pair_send,
    pair_recv,
    small_send,
    small_recv,
    back_send,
    back_recv,
):
    me, core = lax.axis_index("member"), lax.axis_index("pair")
    other = 1 - core
    spares = (spare_a, spare_b, spare_c)
    wide = w_second.shape[1]
    narrow = w_first.shape[1] // 4
    near = wide // 2
    main = wide + narrow
    count = members * ROWS
    holds, tile = own_tile(me)
    extra_here = jnp.logical_or(holds, me == BIAS_AT)

    def rows_of(p):
        return pl.ds(pl.multiple_of(p * ROWS, ROWS), ROWS)

    def first_part(p):
        return (
            pl.ds(pl.multiple_of((p // 4) * ROWS, ROWS), ROWS),
            pl.ds(pl.multiple_of(lax.rem(p, 4) * narrow, narrow), narrow),
        )

    def third_part(e):
        return (
            pl.ds(pl.multiple_of((e // 8) * ROWS, ROWS), ROWS),
            pl.ds(pl.multiple_of(lax.rem(e, 8) * LANES, LANES), LANES),
        )

    def remote(src, dst, send, recv, peer, to_core=None):
        return pltpu.make_async_remote_copy(
            src_ref=src,
            dst_ref=dst,
            send_sem=send,
            recv_sem=recv,
            device_id=(peer, core if to_core is None else to_core),
            device_id_type=MESH,
        )

    def drain(ref, sem):
        pltpu.make_async_copy(ref, ref, sem).wait()

    mine = rows_of(me)
    cols_near, cols_first = pl.ds(0, near), pl.ds(near, narrow)
    cols_far, cols_extra = pl.ds(near + narrow, near), pl.ds(main, LANES)
    cols_early = pl.ds(0, near + narrow)
    left_half, right_half = pl.ds(0, near), pl.ds(near, near)

    barrier = pltpu.get_barrier_semaphore()

    def greet(i, _):
        pl.semaphore_signal(
            barrier, inc=1, device_id=(peer_at(me, i), core), device_id_type=MESH
        )
        return 0

    lax.fori_loop(1, members, greet, 0)
    pl.semaphore_signal(barrier, inc=1, device_id=(me, other), device_id_type=MESH)

    part = samples.shape[0] // 2
    own_cols = pl.ds(pl.multiple_of(core * part, part), part)
    peer_cols = pl.ds(pl.multiple_of(other * part, part), part)
    arriving = (
        (samples, inputs),
        (w_first, first_w),
        (b_first_hbm, b_first),
        (b_second_hbm, b_second),
        (w_second, second_w),
        (w_third_hbm, third_w),
        (observed_hbm.at[:, own_cols], observed),
        (perturb_hbm.at[:, own_cols], perturb),
        (variance_hbm.at[:, own_cols], variance),
    )
    loads = [
        pltpu.make_async_copy(src, dst, load_sem.at[k]) for k, (src, dst) in enumerate(arriving)
    ]
    for load in loads:
        load.start()

    pl.semaphore_wait(barrier, members)

    groups = members // PACE
    units = 2 * groups
    issued = [0]

    def push_unit(u):
        g = u % groups

        def one(i, _):
            p = peer_at(me, i)
            if u < groups:
                remote(
                    w_second.at[rows_of(p), left_half],
                    slab.at[mine, cols_near],
                    send_sem.at[u],
                    recv_sem.at[0],
                    p,
                ).start()
                remote(
                    w_first.at[first_part(p)],
                    slab.at[mine, cols_first],
                    send_sem.at[u],
                    recv_sem.at[0],
                    p,
                ).start()
            else:
                remote(
                    w_second.at[rows_of(p), right_half],
                    slab.at[mine, cols_far],
                    send_sem.at[u],
                    recv_sem.at[1],
                    p,
                ).start()
            return 0

        lax.fori_loop(max(1, g * PACE), (g + 1) * PACE, one, 0)

    def sent_unit(u):
        n = (PACE if u % groups else PACE - 1) * ROWS
        drain(slab.at[pl.ds(0, n), cols_early if u < groups else cols_far], send_sem.at[u])

    def pump(n):
        for u in range(issued[0], min(units, issued[0] + n)):
            push_unit(u)
        issued[0] = min(units, issued[0] + n)

    def push_extra(e, _):
        p = holder(e)
        here = p == me

        @pl.when(here)
        def _():
            pltpu.make_async_copy(
                w_third_hbm.at[third_part(e)], slab.at[mine, cols_extra], recv_extra
            ).start()

        @pl.when(jnp.logical_not(here))
        def _():
            remote(
                w_third_hbm.at[third_part(e)], slab.at[mine, cols_extra], send_extra, recv_extra, p
            ).start()

        return 0

    pump(PLAN[0])
    here_first, here_near, here_far = (
        (w_first.at[first_part(me)], slab.at[mine, cols_first], recv_sem.at[0]),
        (w_second.at[mine, left_half], slab.at[mine, cols_near], recv_sem.at[0]),
        (w_second.at[mine, right_half], slab.at[mine, cols_far], recv_sem.at[1]),
    )
    for own in (here_first, here_near, here_far):
        pltpu.make_async_copy(*own).start()

    for load in loads[:3]:
        load.wait()

    @pl.loop(0, wide // 256)
    def _(n):
        c = pl.ds(pl.multiple_of(n * 256, 256), 256)
        h = jnp.dot(inputs[...], first_w[:, c], preferred_element_type=jnp.float32) * in_scale
        h = h + b_first[:, c].astype(jnp.float32)
        act_own[:, c] = jax.nn.gelu(h, approximate=True).astype(jnp.bfloat16)

    to_pair = remote(act_own, act_peer, pair_send.at[0], pair_recv.at[0], me, other)
    to_pair.start()
    pump(PLAN[1])
    for load in loads[3:]:
        load.wait()
    def bias_rows(i, ref, at):
        bias_wide[at + i : at + i + 1, :] = ref[:, i * LANES : (i + 1) * LANES].astype(jnp.float32)

    for i in range(8):
        bias_rows(i, b_first, 0)
        bias_rows(i, b_second, 8)
    bias[...] = bias_wide[...].astype(jnp.bfloat16)

    to_pair.wait()
    half = second_w.shape[0] // 2
    own_rows = pl.ds(pl.multiple_of(core * half, half), half)
    peer_rows = pl.ds(pl.multiple_of(other * half, half), half)

    @pl.loop(0, wide // 256)
    def _(n):
        c = pl.ds(pl.multiple_of(n * 256, 256), 256)
        h = jnp.dot(act_own[...], second_w[own_rows, c], preferred_element_type=jnp.float32)
        h = h + jnp.dot(act_peer[...], second_w[peer_rows, c], preferred_element_type=jnp.float32)
        h = h * hid_scale + b_second[:, c].astype(jnp.float32)
        second[:, c] = jax.nn.gelu(h, approximate=True).astype(jnp.bfloat16)

    out_t[...] = (
        lax.dot_general(third_w[...], second[...], LAST, preferred_element_type=jnp.float32)
        * hid_scale
    )
    to_pair = remote(out_t.at[:, peer_cols], out_peer, pair_send.at[1], pair_recv.at[1], me, other)
    to_pair.start()
    pump(PLAN[2])
    to_pair.wait()
    pred = out_t[:, own_cols] + out_peer[...]
    resid = observed[...] + jnp.sqrt(variance[...]) * perturb[...] - pred
    tall = pred.shape[0]
    for k in range(2):
        outgoing[k * tall : (k + 1) * tall, 0:LANES] = pred[:, k * LANES : (k + 1) * LANES]
        outgoing[k * tall : (k + 1) * tall, LANES:] = resid[:, k * LANES : (k + 1) * LANES]

    def line(ref, p):
        return ref.at[pl.ds(p, 1), :]

    def scatter_rows(src, dst, k, whole):
        def one(i, _):
            p = peer_at(me, i)
            remote(
                src if whole else line(src, p), line(dst, me), small_send.at[k], small_recv.at[k], p
            ).start()
            return 0

        lax.fori_loop(1, members, one, 0)
        own = src if whole else line(src, me)
        pltpu.make_async_copy(own, line(dst, me), small_recv.at[k]).start()
        pltpu.make_async_copy(own, spares[k], small_send.at[k]).start()

    scatter_rows(outgoing, columns, 0, False)
    pump(PLAN[3])
    drain(columns, small_recv.at[0])
    pred_all, res_all = columns[:, 0:LANES], columns[:, LANES:]
    dev = pred_all - jnp.mean(pred_all, axis=0, keepdims=True)
    var_at = (me // tall) * LANES
    var_rows = variance[:, pl.ds(pl.multiple_of(var_at, LANES), LANES)]
    its_row = lax.broadcasted_iota(jnp.int32, (tall, LANES), 0) == lax.rem(me, tall)
    var_here = jnp.sum(jnp.where(its_row, var_rows, 0.0), axis=0, keepdims=True)
    scaled = dev / var_here
    exact = lax.Precision.HIGHEST
    moments[:, 0:LANES] = lax.dot_general(
        scaled, dev, LAST, precision=exact, preferred_element_type=jnp.float32
    )
    moments[:, LANES:] = lax.dot_general(
        scaled, res_all, LAST, precision=exact, preferred_element_type=jnp.float32
    )

    scatter_rows(moments, partials, 1, False)
    pump(PLAN[4])
    drain(partials, small_recv.at[1])
    row[...] = jnp.sum(partials[...], axis=0, keepdims=True)
    to_pair = remote(row, row_peer, pair_send.at[2], pair_recv.at[2], me, other)
    to_pair.start()
    pump(PLAN[5])
    to_pair.wait()
    row[...] = row[...] + row_peer[...]
    scatter_rows(row, system, 2, True)
    lax.fori_loop(0, THIRDS, push_extra, 0)

    @pl.when(me == BIAS_AT)
    def _():
        pltpu.make_async_copy(bias, slab.at[mine, cols_extra], recv_extra).start()

    @pl.when(me != BIAS_AT)
    def _():
        remote(bias, slab.at[mine, cols_extra], send_extra, recv_extra, BIAS_AT).start()

    pump(units)

    at = lax.broadcasted_iota(jnp.int32, (members, count), 1) // ROWS
    who = lax.broadcasted_iota(jnp.int32, (members, count), 0)
    spread[...] = jnp.where(at == who, 1.0, 0.0).astype(jnp.bfloat16)
    drain(system, small_recv.at[2])

    d0 = lax.broadcasted_iota(jnp.int32, (members, members), 0)
    d1 = lax.broadcasted_iota(jnp.int32, (members, members), 1)
    system[:, 0:members] = system[:, 0:members] + jnp.where(d0 == d1, float(members), 0.0)
    lane = lax.broadcasted_iota(jnp.int32, (1, 2 * members), 1)

    def eliminate(i, _):
        now = system[...]
        top = system[pl.ds(i, 1), :]
        col = jnp.sum(jnp.where(lane == i, now, 0.0), axis=1, keepdims=True)
        pivot = jnp.sum(jnp.where(lane == i, top, 0.0), axis=1, keepdims=True)
        top = top / pivot
        system[...] = now - col * top
        system[pl.ds(i, 1), :] = top
        return 0

    lax.fori_loop(0, members, eliminate, 0)
    gain = system[:, members:].astype(jnp.bfloat16)
    peers = GROUP // ROWS

    @pl.loop(0, count // GROUP)
    def _(g):
        ir = lax.broadcasted_iota(jnp.int32, (GROUP, members), 0) // ROWS + g * peers
        jj = lax.broadcasted_iota(jnp.int32, (GROUP, members), 1)
        pick = jnp.where(peer_at(me, ir) == jj, 1.0, 0.0).astype(jnp.bfloat16)
        spread_out = lax.dot_general(pick, gain, LAST, preferred_element_type=jnp.float32)
        out_rows = pl.ds(pl.multiple_of(g * GROUP, GROUP), GROUP)
        weight_sums[out_rows, :] = jnp.sum(spread_out, axis=1, keepdims=True)
        spread_out = spread_out.astype(jnp.bfloat16)

        @pl.loop(0, count // 512)
        def _(q):
            c = pl.ds(pl.multiple_of(q * 512, 512), 512)
            full = jnp.dot(spread_out, spread[:, c], preferred_element_type=jnp.float32)
            r0 = lax.broadcasted_iota(jnp.int32, (GROUP, 512), 0) % ROWS
            r1 = lax.broadcasted_iota(jnp.int32, (GROUP, 512), 1) % ROWS
            weights[out_rows, c] = jnp.where(r0 == r1, full, 0.0).astype(jnp.bfloat16)

    tr = lax.broadcasted_iota(jnp.int32, (ROWS, count), 1) % ROWS
    tw = lax.broadcasted_iota(jnp.int32, (ROWS, count), 0)
    same = jnp.where(tr == tw, 1.0, 0.0).astype(jnp.bfloat16)

    def mean_of(c):
        avg[:, c] = jnp.dot(same, slab[:, c], preferred_element_type=jnp.float32) * (1.0 / members)

    def mix(g, c, width):
        out_rows = pl.ds(pl.multiple_of(g * GROUP, GROUP), GROUP)
        acc = jnp.dot(weights[out_rows, :], slab[:, c], preferred_element_type=jnp.float32)
        means = jnp.broadcast_to(avg[:, c][None], (peers, ROWS, width)).reshape(GROUP, width)
        mixed[out_rows, c] = (acc - weight_sums[out_rows, :] * means).astype(jnp.bfloat16)

    def tiles(lo, hi, do):
        @pl.loop(lo // 256, hi // 256)
        def _(n):
            do(pl.ds(pl.multiple_of(n * 256, 256), 256))

    targets = (
        (cols_near, new_second.at[mine, left_half]),
        (cols_first, new_first.at[first_part(me)]),
        (cols_far, new_second.at[mine, right_half]),
        (cols_extra, new_third.at[third_part(tile)]),
        (cols_extra, bias_back),
    )

    def send_back(i, k):
        c, dst = targets[k]
        send = back_send.at[k]
        remote(mixed.at[rows_of(i), c], dst, send, back_recv.at[k], peer_at(me, i)).start()

    def keep_own(k):
        c, dst = targets[k]
        pltpu.make_async_copy(mixed.at[pl.ds(0, ROWS), c], dst, back_recv.at[k]).start()

    def mix_and_send(early):
        def send(i):
            for k in (0, 1) if early else (2,):
                send_back(i, k)
            if not early:
                pl.when(holds)(lambda: send_back(i, 3))
                pl.when(me == BIAS_AT)(lambda: send_back(i, 4))

        @pl.loop(0, count // GROUP)
        def _(g):
            if early:
                tiles(0, near + narrow, lambda c: mix(g, c, 256))
            else:
                tiles(near + narrow, main, lambda c: mix(g, c, 256))
                pl.when(extra_here)(lambda: mix(g, cols_extra, LANES))

            @pl.loop(jnp.where(g == 0, 1, g * peers), (g + 1) * peers)
            def _(i):
                send(i)

        for k in (0, 1) if early else (2,):
            keep_own(k)
        if not early:
            pl.when(holds)(lambda: keep_own(3))
            pl.when(me == BIAS_AT)(lambda: keep_own(4))

    drain(slab.at[:, cols_early], recv_sem.at[0])
    tiles(0, near + narrow, mean_of)
    mix_and_send(True)
    drain(slab.at[:, cols_far], recv_sem.at[1])
    pl.when(extra_here)(lambda: drain(slab.at[:, cols_extra], recv_extra))
    tiles(near + narrow, main, mean_of)
    pl.when(extra_here)(lambda: mean_of(cols_extra))
    mix_and_send(False)

    others = pl.ds(0, (members - 1) * ROWS)
    for u in range(units):
        sent_unit(u)
    for k in range(3):
        drain(outgoing, small_send.at[k])

    @pl.when(extra_here)
    def _():
        drain(slab.at[pl.ds(0, THIRDS * ROWS), cols_extra], send_extra)

    @pl.when(jnp.logical_not(extra_here))
    def _():
        drain(slab.at[pl.ds(0, (THIRDS + 1) * ROWS), cols_extra], send_extra)

    for k in range(3):
        drain(mixed.at[others, targets[k][0]], back_send.at[k])
    pl.when(holds)(lambda: drain(mixed.at[others, cols_extra], back_send.at[3]))
    pl.when(me == BIAS_AT)(lambda: drain(mixed.at[others, cols_extra], back_send.at[4]))
    drain(new_second.at[:, left_half], back_recv.at[0])
    drain(new_first, back_recv.at[1])
    drain(bias_back, back_recv.at[4])
    bias_wide[...] = bias_back[...].astype(jnp.float32)
    for i in range(8):
        c = slice(i * LANES, (i + 1) * LANES)
        new_bfirst[:, c] = bias_wide[i : i + 1, :].astype(jnp.bfloat16)
        new_bsecond[:, c] = bias_wide[8 + i : 9 + i, :].astype(jnp.bfloat16)
    drain(new_third, back_recv.at[3])
    drain(new_second.at[:, right_half], back_recv.at[2])


def store_kernel(*refs):
    n = (len(refs) - 1) // 2
    sem = refs[-1]
    copies = []
    for src, dst in zip(refs[:n], refs[n : 2 * n]):
        cuts = max(1, src.shape[0] // 512)
        rows = src.shape[0] // cuts
        for k in range(cuts):
            at = pl.ds(k * rows, rows)
            copies.append(
                pltpu.make_async_copy(src.at[at, :], dst.at[at, :], sem.at[len(copies)])
            )
    for copy in copies:
        copy.start()
    for copy in copies:
        copy.wait()


def body(samples, w_first, b_first, w_second, b_second, w_third, observed, perturb, variance):
    members = lax.axis_size("member")
    in_scale = samples.shape[1] ** (-0.5)
    hid_scale = w_second.shape[1] ** (-0.5)
    first_w, second_w, third_w = w_first[0], w_second[0], w_third[0].T
    count = members * ROWS
    wide = second_w.shape[1] + first_w.shape[1] // 4 + LANES
    batch, hidden, outs = samples.shape[0], second_w.shape[1], third_w.shape[0]
    anywhere = pl.BlockSpec(memory_space=pl.ANY)
    onchip = pl.BlockSpec(memory_space=pltpu.VMEM)
    dma = pltpu.SemaphoreType.DMA
    low, full = jnp.bfloat16, jnp.float32
    shapes = (first_w, b_first, second_w, b_second, third_w)
    mixed = pl.pallas_call(
        functools.partial(kernel, members, in_scale, hid_scale),
        out_shape=[pltpu.VMEM(a.shape, a.dtype) for a in shapes],
        in_specs=[anywhere] * 9,
        out_specs=[onchip] * 5,
        scratch_shapes=[
            pltpu.VMEM((count, wide), low),
            pltpu.VMEM((count, wide), low),
            pltpu.VMEM((count, count), low),
            pltpu.VMEM((count, 1), full),
            pltpu.VMEM((members, count), low),
            pltpu.VMEM((ROWS, wide), full),
            pltpu.VMEM(samples.shape, low),
            pltpu.VMEM(first_w.shape, low),
            pltpu.VMEM(second_w.shape, low),
            pltpu.VMEM(third_w.shape, low),
            pltpu.VMEM(b_first.shape, low),
            pltpu.VMEM(b_second.shape, low),
            pltpu.VMEM((outs, batch // 2), full),
            pltpu.VMEM((outs, batch // 2), full),
            pltpu.VMEM((outs, batch // 2), full),
            pltpu.VMEM((batch, hidden), low),
            pltpu.VMEM((batch, hidden), low),
            pltpu.VMEM((batch, hidden), low),
            pltpu.VMEM((outs, batch), full),
            pltpu.VMEM((outs, batch // 2), full),
            pltpu.VMEM((members, 2 * LANES), full),
            pltpu.VMEM((members, 2 * LANES), full),
            pltpu.VMEM((members, 2 * LANES), full),
            pltpu.VMEM((members, 2 * LANES), full),
            pltpu.VMEM((1, 2 * LANES), full),
            pltpu.VMEM((1, 2 * LANES), full),
            pltpu.VMEM((members, 2 * LANES), full),
            pltpu.VMEM((1, 2 * LANES), full),
            pltpu.VMEM((1, 2 * LANES), full),
            pltpu.VMEM((1, 2 * LANES), full),
            pltpu.VMEM((ROWS, LANES), full),
            pltpu.VMEM((ROWS, LANES), low),
            pltpu.VMEM((ROWS, LANES), low),
            dma((9,)),
            dma((2 * members // PACE,)),
            dma((2,)),
            dma,
            dma,
            dma((3,)),
            dma((3,)),
            dma((3,)),
            dma((3,)),
            dma((5,)),
            dma((5,)),
        ],
        compiler_params=pltpu.CompilerParams(
            collective_id=0, has_side_effects=True, vmem_limit_bytes=50 << 20
        ),
    )(
        *(
            pltpu.with_memory_space_constraint(a, pltpu.HBM)
            for a in (
                samples,
                first_w,
                b_first,
                second_w,
                b_second,
                third_w,
                observed.T,
                perturb[0].T,
                variance.T,
            )
        )
    )
    new_first, new_bfirst, new_second, new_bsecond, new_third = pl.pallas_call(
        store_kernel,
        out_shape=[jax.ShapeDtypeStruct(a.shape, a.dtype) for a in shapes],
        in_specs=[anywhere] * 5,
        out_specs=[anywhere] * 5,
        scratch_shapes=[dma((8,))],
        compiler_params=pltpu.CompilerParams(vmem_limit_bytes=1 << 20),
    )(*(pltpu.with_memory_space_constraint(a, pltpu.VMEM) for a in mixed))
    return (new_first[None], new_bfirst, new_second[None], new_bsecond, new_third.T[None])


def solution(mesh):
    in_specs = (
        P(),
        P("member", None, "pair"),
        P("member", "pair"),
        P("member", None, "pair"),
        P("member", "pair"),
        P("member", "pair", None),
        P(),
        P("member", None, None),
        P(),
    )
    out_specs = (
        P("member", None, "pair"),
        P("member", "pair"),
        P("member", None, "pair"),
        P("member", "pair"),
        P("member", "pair", None),
    )
    return jax.shard_map(body, mesh=mesh, in_specs=in_specs, out_specs=out_specs, check_vma=False)
```

time: 292 us -> 264 us (0.904); the launches traced: 288 us -> 264 us
  local copies, waits for them, and re-layouts: 14.7 us -> 0 us
  Pallas kernels: 273 us -> 263 us
    unnamed x21 -> x0, local copies, waits for them, and re-layouts: 14.7 us -> none
    pallas_call x1, Pallas kernels: 273 us -> 260 us  [body(): pl.pallas_call(functools.partial(kernel, members, in_scale, hid_scale), o...]
where the time goes in v3:
time: 264 us
  Pallas kernels  263 us (100%)
    pallas_call x1, Pallas kernels, body(): pl.pallas_call(functools.partial(kernel, members, in_scale, hid_scale), o...  260 us

profile of v3, /device:TPU:30, one launch (start us, length us, event | category | flops | bytes accessed | tf_op | source)
XLA Modules:
  0.0 263.5 jit_solution(4105817453816879845)
XLA Ops:
  0.6 260.4 %shard_map.128 = (bf16[512,1024]{1,0:T(8,128)(2,1)S(1)}, bf16[1,1024]{1,0:T(2,128)(2,1)S(1)}, bf16[2048,1024]{1,0:T(8,128)(2,1)S(1)}, bf16[1,1024]{1,0:T(2,128)(2,1)S(1)}, bf16[64,1024]{1,0:T(8,128)(2,1)S(1)}) custom-call(bf16[512,512]{1,0:T(8,128)(2,1)} %samples.1, bf16[512,1024]{1,0:T(8,128)(2,1)} %bitcast.16, bf16[1,1024]{1,0:T(2,128)(2,1)} %b_first_hbm.1, ...), custom_call_target="tpu_custom_call" | custom-call | tf_op jit(solution)/shard_map/pallas_call | solution.py:530
  261.1 2.4 shard_map.129

commit v4 on v3

--- a/solution.py
+++ b/solution.py
@@ -11,27 +11,38 @@
 ROWS = 16
 LANES = 128
 THIRDS = 32
-BIAS_AT = 4
+BIAS_AT = 1
 PACE = 8
-PLAN = (6, 2, 0, 2, 2, 0)
+PLAN = (6, 2, 0, 2, 0, 2, 2, 1, 2)
+RING = 8
 GROUP = 256
 LAST = (((1,), (1,)), ((), ()))
 
 
+def label(member):
+    y, z, x = member // 32, (member >> 2) & 7, member & 3
+    return y * 32 + x * 8 + z
+
+
+def member_of(number):
+    y, x, z = number >> 5, (number >> 3) & 3, number & 7
+    return y * 32 + z * 4 + x
+
+
 def peer_at(me, i):
-    y, z, x = me // 32, lax.rem(me // 4, 8), lax.rem(me, 4)
+    y, x, z = me >> 5, (me >> 3) & 3, me & 7
     dz, dx, dy = i & 7, (i >> 3) & 3, i >> 5
-    return ((y + dy) & 3) * 32 + ((z + dz) & 7) * 4 + ((x + dx) & 3)
+    return ((y + dy) & 3) * 32 + ((x + dx) & 3) * 8 + ((z + dz) & 7)
 
 
 def holder(e):
-    y, x = e // 8, lax.rem(e // 2, 4)
-    return y * 32 + (lax.rem(x + y, 4) + 4 * lax.rem(e, 2)) * 4 + x
+    ring = e // 2
+    return ring * 8 + (((ring >> 2) + ring) & 3) + 4 * (e & 1)
 
 
 def own_tile(me):
-    y, z, x = me // 32, lax.rem(me // 4, 8), lax.rem(me, 4)
-    return lax.rem(z, 4) == lax.rem(x + y, 4), y * 8 + x * 2 + z // 4
+    ring, z = me >> 3, me & 7
+    return (z & 3) == (((ring >> 2) + ring) & 3), ring * 2 + (z >> 2)
 
 
 def kernel(
@@ -76,8 +87,12 @@
     columns,
     moments,
     partials,
+    block,
+    block_in,
     row,
     row_peer,
+    block_out,
+    blocks_out,
     system,
     spare_a,
     spare_b,
@@ -97,9 +112,9 @@
     back_send,
     back_recv,
 ):
-    me, core = lax.axis_index("member"), lax.axis_index("pair")
+    me, core = label(lax.axis_index("member")), lax.axis_index("pair")
+    plane, spot = me >> 3, me & 7
     other = 1 - core
-    spares = (spare_a, spare_b, spare_c)
     wide = w_second.shape[1]
     narrow = w_first.shape[1] // 4
     near = wide // 2
@@ -129,7 +144,7 @@
             dst_ref=dst,
             send_sem=send,
             recv_sem=recv,
-            device_id=(peer, core if to_core is None else to_core),
+            device_id=(member_of(peer), core if to_core is None else to_core),
             device_id_type=MESH,
         )
 
@@ -146,12 +161,15 @@
 
     def greet(i, _):
         pl.semaphore_signal(
-            barrier, inc=1, device_id=(peer_at(me, i), core), device_id_type=MESH
+            barrier,
+            inc=1,
+            device_id=(member_of(peer_at(me, i)), core),
+            device_id_type=MESH,
         )
         return 0
 
     lax.fori_loop(1, members, greet, 0)
-    pl.semaphore_signal(barrier, inc=1, device_id=(me, other), device_id_type=MESH)
+    pl.semaphore_signal(barrier, inc=1, device_id=(member_of(me), other), device_id_type=MESH)
 
     part = samples.shape[0] // 2
     own_cols = pl.ds(pl.multiple_of(core * part, part), part)
@@ -294,27 +312,45 @@
     pred = out_t[:, own_cols] + out_peer[...]
     resid = observed[...] + jnp.sqrt(variance[...]) * perturb[...] - pred
     tall = pred.shape[0]
+    planes = members // RING
     for k in range(2):
-        outgoing[k * tall : (k + 1) * tall, 0:LANES] = pred[:, k * LANES : (k + 1) * LANES]
-        outgoing[k * tall : (k + 1) * tall, LANES:] = resid[:, k * LANES : (k + 1) * LANES]
+        at, c = slice(k * tall, (k + 1) * tall), slice(k * LANES, (k + 1) * LANES)
+        outgoing[at, 0:LANES] = pred[:, c]
+        outgoing[at, LANES:] = resid[:, c]
+
+    def over_planes(part_for, dst, k):
+        def one(d, _):
+            to = (plane + d) & (planes - 1)
+            remote(
+                part_for(to), dst.at[plane], small_send.at[k], small_recv.at[k], to * RING + spot
+            ).start()
+            return 0
+
+        lax.fori_loop(1, planes, one, 0)
+        pltpu.make_async_copy(part_for(plane), dst.at[plane], small_recv.at[k]).start()
+
+    def over_ring(part_for, place, k):
+        def one(d, _):
+            to = (spot + d) & (RING - 1)
+            remote(
+                part_for(to), place, small_send.at[k], small_recv.at[k], plane * RING + to
+            ).start()
+            return 0
+
+        lax.fori_loop(1, RING, one, 0)
+        pltpu.make_async_copy(part_for(spot), place, small_recv.at[k]).start()
 
     def line(ref, p):
         return ref.at[pl.ds(p, 1), :]
 
-    def scatter_rows(src, dst, k, whole):
-        def one(i, _):
-            p = peer_at(me, i)
-            remote(
-                src if whole else line(src, p), line(dst, me), small_send.at[k], small_recv.at[k], p
-            ).start()
-            return 0
-
-        lax.fori_loop(1, members, one, 0)
-        own = src if whole else line(src, me)
-        pltpu.make_async_copy(own, line(dst, me), small_recv.at[k]).start()
-        pltpu.make_async_copy(own, spares[k], small_send.at[k]).start()
-
-    scatter_rows(outgoing, columns, 0, False)
+    def scatter_row(i, _):
+        p = peer_at(me, i)
+        remote(line(outgoing, p), line(columns, me), small_send.at[0], small_recv.at[0], p).start()
+        return 0
+
+    lax.fori_loop(1, members, scatter_row, 0)
+    pltpu.make_async_copy(line(outgoing, me), line(columns, me), small_recv.at[0]).start()
+    pltpu.make_async_copy(line(outgoing, me), spare_c, small_send.at[0]).start()
     pump(PLAN[3])
     drain(columns, small_recv.at[0])
     pred_all, res_all = columns[:, 0:LANES], columns[:, LANES:]
@@ -325,23 +361,31 @@
     var_here = jnp.sum(jnp.where(its_row, var_rows, 0.0), axis=0, keepdims=True)
     scaled = dev / var_here
     exact = lax.Precision.HIGHEST
-    moments[:, 0:LANES] = lax.dot_general(
-        scaled, dev, LAST, precision=exact, preferred_element_type=jnp.float32
-    )
-    moments[:, LANES:] = lax.dot_general(
-        scaled, res_all, LAST, precision=exact, preferred_element_type=jnp.float32
-    )
-
-    scatter_rows(moments, partials, 1, False)
-    pump(PLAN[4])
-    drain(partials, small_recv.at[1])
-    row[...] = jnp.sum(partials[...], axis=0, keepdims=True)
+    for at, with_all in ((slice(0, LANES), dev), (slice(LANES, 2 * LANES), res_all)):
+        sums = lax.dot_general(
+            scaled, with_all, LAST, precision=exact, preferred_element_type=jnp.float32
+        )
+        moments[:, :, at] = sums.reshape(planes, RING, LANES)
+
+    over_planes(lambda to: moments.at[to], partials, 2)
+    pump(PLAN[5])
+    drain(partials, small_recv.at[2])
+    block[...] = jnp.sum(partials[...], axis=0)
+    over_ring(lambda to: line(block, to), line(block_in, spot), 3)
+    pltpu.make_async_copy(line(block, spot), spare_a, small_send.at[3]).start()
+    pump(PLAN[6])
+    drain(block_in, small_recv.at[3])
+    row[...] = jnp.sum(block_in[...], axis=0, keepdims=True)
     to_pair = remote(row, row_peer, pair_send.at[2], pair_recv.at[2], me, other)
     to_pair.start()
-    pump(PLAN[5])
+    pump(PLAN[7])
     to_pair.wait()
     row[...] = row[...] + row_peer[...]
-    scatter_rows(row, system, 2, True)
+    over_ring(lambda to: row, line(block_out, spot), 4)
+    pltpu.make_async_copy(row, spare_b, small_send.at[4]).start()
+    pump(PLAN[8])
+    drain(block_out, small_recv.at[4])
+    over_planes(lambda to: block_out, blocks_out, 5)
     lax.fori_loop(0, THIRDS, push_extra, 0)
 
     @pl.when(me == BIAS_AT)
@@ -357,11 +401,13 @@
     at = lax.broadcasted_iota(jnp.int32, (members, count), 1) // ROWS
     who = lax.broadcasted_iota(jnp.int32, (members, count), 0)
     spread[...] = jnp.where(at == who, 1.0, 0.0).astype(jnp.bfloat16)
-    drain(system, small_recv.at[2])
+    drain(blocks_out, small_recv.at[5])
 
     d0 = lax.broadcasted_iota(jnp.int32, (members, members), 0)
     d1 = lax.broadcasted_iota(jnp.int32, (members, members), 1)
-    system[:, 0:members] = system[:, 0:members] + jnp.where(d0 == d1, float(members), 0.0)
+    summed_up = blocks_out[...].reshape(members, 2 * members)
+    system[:, 0:members] = summed_up[:, 0:members] + jnp.where(d0 == d1, float(members), 0.0)
+    system[:, members:] = summed_up[:, members:]
     lane = lax.broadcasted_iota(jnp.int32, (1, 2 * members), 1)
 
     def eliminate(i, _):
@@ -469,8 +515,11 @@
     others = pl.ds(0, (members - 1) * ROWS)
     for u in range(units):
         sent_unit(u)
-    for k in range(3):
-        drain(outgoing, small_send.at[k])
+    drain(outgoing, small_send.at[0])
+    for k in (2, 5):
+        drain(moments.at[pl.ds(0, planes - 1)], small_send.at[k])
+    for k in (3, 4):
+        drain(block, small_send.at[k])
 
     @pl.when(extra_here)
     def _():
@@ -526,6 +575,7 @@
     onchip = pl.BlockSpec(memory_space=pltpu.VMEM)
     dma = pltpu.SemaphoreType.DMA
     low, full = jnp.bfloat16, jnp.float32
+    by_plane = (members // RING, RING, 2 * LANES)
     shapes = (first_w, b_first, second_w, b_second, third_w)
     mixed = pl.pallas_call(
         functools.partial(kernel, members, in_scale, hid_scale),
@@ -555,10 +605,14 @@
             pltpu.VMEM((outs, batch // 2), full),
             pltpu.VMEM((members, 2 * LANES), full),
             pltpu.VMEM((members, 2 * LANES), full),
-            pltpu.VMEM((members, 2 * LANES), full),
-            pltpu.VMEM((members, 2 * LANES), full),
+            pltpu.VMEM(by_plane, full),
+            pltpu.VMEM(by_plane, full),
+            pltpu.VMEM((RING, 2 * LANES), full),
+            pltpu.VMEM((RING, 2 * LANES), full),
             pltpu.VMEM((1, 2 * LANES), full),
             pltpu.VMEM((1, 2 * LANES), full),
+            pltpu.VMEM((RING, 2 * LANES), full),
+            pltpu.VMEM(by_plane, full),
             pltpu.VMEM((members, 2 * LANES), full),
             pltpu.VMEM((1, 2 * LANES), full),
             pltpu.VMEM((1, 2 * LANES), full),
@@ -573,8 +627,8 @@
             dma,
             dma((3,)),
             dma((3,)),
-            dma((3,)),
-            dma((3,)),
+            dma((6,)),
+            dma((6,)),
             dma((5,)),
             dma((5,)),
         ],

time: 264 us -> 265 us (level)
  no operation moved by 1% of the time
where the time goes in v4:
time: 265 us; the launch traced here: 264 us
  Pallas kernels  263 us (99%)
    pallas_call x1, Pallas kernels, body(): pl.pallas_call(functools.partial(kernel, members, in_scale, hid_scale), o...  260 us

profile of v4, /device:TPU:30, one launch (start us, length us, event | category | flops | bytes accessed | tf_op | source)
XLA Modules:
  0.0 263.5 jit_solution(13184038857580157745)
XLA Ops:
  0.6 260.5 %shard_map.128 = (bf16[512,1024]{1,0:T(8,128)(2,1)S(1)}, bf16[1,1024]{1,0:T(2,128)(2,1)S(1)}, bf16[2048,1024]{1,0:T(8,128)(2,1)S(1)}, bf16[1,1024]{1,0:T(2,128)(2,1)S(1)}, bf16[64,1024]{1,0:T(8,128)(2,1)S(1)}) custom-call(bf16[512,512]{1,0:T(8,128)(2,1)} %samples.1, bf16[512,1024]{1,0:T(8,128)(2,1)} %bitcast.16, bf16[1,1024]{1,0:T(2,128)(2,1)} %b_first_hbm.1, ...), custom_call_target="tpu_custom_call" | custom-call | tf_op jit(solution)/shard_map/pallas_call | solution.py:580
  261.1 2.4 shard_map.129
